TPU v7x, 32 devices: a whole 2x2x4 slice. The times are simulated.
32 devices in a mesh: clips: 2 (over x), tm: 8 (over z, y), cols: 2 (over core).
Axes of the slice: x: 2, y: 2, z: 4, core: 2. Of those that a mesh axis runs over, the one named last changes fastest.
Arguments:
- video: bfloat16 [64, 32, 32, 512], P(('clips', 'tm'), None, 'cols'), parts along dimension 0, may hold values from -6 to 6
- w_time: bfloat16 [3, 512, 512], replicated, may hold values from -0.15625 to 0.15625
- b_time: float32 [512], replicated, may hold values from -3 to 3
- w_down: bfloat16 [3, 512, 512], replicated, may hold values from -0.15625 to 0.15625
- b_down: float32 [512], replicated, may hold values from -3 to 3
- w_space: bfloat16 [9, 512, 512], replicated, may hold values from -0.09375 to 0.09375
- b_space: float32 [512], replicated, may hold values from -3 to 3
- gain: float32 [512], replicated, may hold values from 0.1 to 1.9
- w_query: bfloat16 [512, 512], replicated, may hold values from -30 to 30
- w_key: bfloat16 [512, 512], replicated, may hold values from -0.25 to 0.25
- w_value: bfloat16 [512, 512], replicated, may hold values from -0.25 to 0.25
- w_out: bfloat16 [512, 512], replicated, may hold values from -0.25 to 0.25
Outputs:
- encoded: bfloat16 [32, 32, 32, 512], P(('clips', 'tm'), None, 'cols'), parts along dimension 0
There are 2 independent parts, one for each index of `clips`. A program takes and returns all parts, laid end to end along the dimension named above; an argument that names none is the same for every part. Nothing has to cross between parts.
All inputs are finite; a program needn't handle non-finite values.
Results may differ from a plain program's by a relative error of at most 0.019.
The roundings to bfloat16 on the way count: a program that leaves them out, or rounds other values in their place, can miss the bound.
Values may be sent and summed in bfloat16 or wider, within the bound.
A program may use at most 64 MiB of HBM per device.

v0:
```python
from functools import partial

import jax
import jax.numpy as jnp
from jax import lax
from jax.sharding import PartitionSpec as P

epsilon = 1e-06


def passed_along(value, axis, steps):
    count = lax.axis_size(axis)
    first, last = (max(0, -steps), min(count, count - steps))
    return lax.ppermute(value, axis, [(source, source + steps) for source in range(first, last)])


def padded(x, sides, width):
    for axis, dim in sides:
        devices, length = (lax.axis_size(axis), x.shape[dim])
        up = [(i, (i + 1) % devices) for i in range(devices - 1)]
        down = [(j, i) for i, j in up]
        last = lax.slice_in_dim(x, length - width, length, axis=dim)
        first = lax.slice_in_dim(x, 0, width, axis=dim)
        before = lax.ppermute(last, axis, up)
        after = lax.ppermute(first, axis, down)
        x = jnp.concatenate([before, x, after], axis=dim)
    return x


def attend(sequence, gain, w_query, w_key, w_value, w_out):
    frames, pixels, channels = sequence.shape
    wide = sequence.astype(jnp.float32)
    scale = lax.rsqrt(jnp.mean(wide * wide, axis=-1, keepdims=True) + epsilon)
    normed = (wide * scale * gain).astype(jnp.bfloat16).reshape(-1, channels)
    query = (
        jnp.dot(normed, w_query, preferred_element_type=jnp.float32)
        .astype(jnp.bfloat16)
        .reshape(frames, pixels, channels)
    )
    key = (
        jnp.dot(normed, w_key, preferred_element_type=jnp.float32)
        .astype(jnp.bfloat16)
        .reshape(frames, pixels, channels)
    )
    value = (
        jnp.dot(normed, w_value, preferred_element_type=jnp.float32)
        .astype(jnp.bfloat16)
        .reshape(frames, pixels, channels)
    )
    scores = jnp.einsum(
        "spc,tpc->pst", query, key, preferred_element_type=jnp.float32
    ) * channels ** (-0.5)
    steps = jnp.arange(frames)
    allowed = steps[None, :] <= steps[:, None]
    scores = jnp.where(allowed[None], scores, -1e30)
    largest = jnp.max(scores, axis=-1, keepdims=True)
    probs = jnp.exp(scores - largest)
    probs = (probs / jnp.sum(probs, axis=-1, keepdims=True)).astype(jnp.bfloat16)
    context = jnp.einsum("pst,tpc->spc", probs, value, preferred_element_type=jnp.float32).astype(
        jnp.bfloat16
    )
    mixed = jnp.dot(
        context.reshape(-1, channels), w_out, preferred_element_type=jnp.float32
    ).reshape(frames, pixels, channels)
    return (wide + mixed).astype(jnp.bfloat16)


def attend_group(block, attention):
    frames, single, pixels, channels = block.shape
    result = attention(block.reshape(frames, single * pixels, channels))
    return result.reshape(frames, single, pixels, channels)


def temporal(extended, weights, bias, first, count):
    _, height, strip, channels = extended.shape
    summed = jnp.zeros((count * height * strip, channels), jnp.float32) + bias
    for offset in range(3):
        window = extended[first - offset : first - offset + count]
        summed = summed + jnp.dot(
            window.reshape(-1, channels), weights[offset], preferred_element_type=jnp.float32
        )
    return summed.reshape(count, height, strip, channels)


def per_device(
    video, w_time, b_time, w_down, b_down, w_space, b_space, gain, w_query, w_key, w_value, w_out
):
    frames, height, strip, channels = video.shape
    before = passed_along(video[frames - 2 :], "tm", 1)
    extended = jnp.concatenate([before, video], 0)
    summed = temporal(extended, w_time, b_time, 2, frames)
    lifted = (video.astype(jnp.float32) + jax.nn.silu(summed)).astype(jnp.bfloat16)
    carried = passed_along(lifted[frames - 1 :], "tm", 1)
    lifted_ext = jnp.concatenate([carried, lifted], 0)
    halves = frames // 2
    taps = [lifted_ext[2 : frames + 1 : 2], lifted_ext[1:frames:2], lifted_ext[0 : frames - 1 : 2]]
    summed = jnp.zeros((halves * height * strip, channels), jnp.float32) + b_down
    for offset in range(3):
        summed = summed + jnp.dot(
            taps[offset].reshape(-1, channels), w_down[offset], preferred_element_type=jnp.float32
        )
    reduced = summed.reshape(halves, height, strip, channels).astype(jnp.bfloat16)
    framed = padded(reduced, (("cols", 2),), 1)
    framed = jnp.pad(framed, ((0, 0), (1, 1), (0, 0), (0, 0)))
    summed = jnp.zeros((halves * height * strip, channels), jnp.float32) + b_space
    for row_tap in range(3):
        for col_tap in range(3):
            window = framed[:, row_tap : row_tap + height, col_tap : col_tap + strip]
            summed = summed + jnp.dot(
                window.reshape(-1, channels),
                w_space[3 * row_tap + col_tap],
                preferred_element_type=jnp.float32,
            )
    spatial = (
        reduced.astype(jnp.float32) + jax.nn.silu(summed.reshape(halves, height, strip, channels))
    ).astype(jnp.bfloat16)
    flattened = spatial.reshape(halves, height * strip, channels)
    attention = partial(
        attend, gain=gain, w_query=w_query, w_key=w_key, w_value=w_value, w_out=w_out
    )
    owners = lax.axis_size("tm")
    grouped = flattened.reshape(halves, owners, height * strip // owners, channels)
    worker = partial(attend_group, attention=attention)
    attended_four = worker(lax.all_to_all(grouped, "tm", split_axis=1, concat_axis=0, tiled=True))
    attended = attended_four.reshape(halves * owners, height * strip // owners, channels)
    returned = lax.all_to_all(attended, "tm", split_axis=0, concat_axis=1, tiled=True)
    return returned.reshape(halves, height, strip, channels)


def solution(mesh):
    return jax.shard_map(
        per_device,
        mesh=mesh,
        in_specs=(
            P(("clips", "tm"), None, "cols", None),
            P(),
            P(),
            P(),
            P(),
            P(),
            P(),
            P(),
            P(),
            P(),
            P(),
            P(),
        ),
        out_specs=P(("clips", "tm"), None, "cols", None),
        check_vma=False,
    )
```

profile of v0, /device:TPU:0, one launch (start us, length us, event | category | flops | bytes accessed | tf_op | source)
XLA Modules:
  0.0 141.1 jit_solution(7019561361036604672)
XLA Ops:
  0.0 1.4 %slice.103 = bf16[2,32,16,512]{3,2,1,0:T(8,128)(2,1)S(1)} slice(bf16[4,32,16,512]{3,2,1,0:T(8,128)(2,1)} %param.12), slice={[2:4], [0:32], [0:16], [0:512]} | slice | bytes 2097152 | tf_op jit(solution)/shard_map/slice | solution.py:89
  1.5 5.0 %collective-permute-start = (bf16[2,32,16,512]{3,2,1,0:T(8,128)(2,1)S(1)}, bf16[2,32,16,512]{3,2,1,0:T(8,128)(2,1)S(1)}, u32[]{:S(2)}, u32[]{:S(2)}) collective-permute-start(bf16[2,32,16,512]{3,2,1,0:T(8,128)(2,1)S(1)} %slice.103), channel_id=1, source_target_pairs={{0,2},{2,4},{4,6},{6,8},{8,10},{10,12},{12,14},{1,3},{3,5},{5,7},{... | collective-permute-start | bytes 3145736 | tf_op jit(solution)/shard_map/ppermute | solution.py:14
  6.4 2.3 %fusion.46 = f32[2048,512]{1,0:T(8,128)S(1)} fusion(bf16[2048,512]{1,0:T(8,128)(2,1)S(1)} %bitcast.117, bf16[3,512,512]{2,1,0:T(8,128)(2,1)} %param.13), kind=kOutput, calls=%fused_computation.63 | convolution fusion | flops 1073741824 | bytes 6815744 | tf_op jit(solution)/shard_map/dot_general | solution.py:79
  8.7 20.0 %collective-permute-done = bf16[2,32,16,512]{3,2,1,0:T(8,128)(2,1)S(1)} collective-permute-done((bf16[2,32,16,512]{3,2,1,0:T(8,128)(2,1)S(1)}, bf16[2,32,16,512]{3,2,1,0:T(8,128)(2,1)S(1)}, u32[]{:S(2)}, u32[]{:S(2)}) %collective-permute-start) | collective-permute-done | bytes 1048608 | tf_op jit(solution)/shard_map/ppermute | solution.py:14
  28.8 0.2 constant_dynamic-update-slice_fusion
  29.0 0.6 fusion.65
  29.6 0.8 copy-done.2
  30.4 1.3 fusion.44
  31.7 1.4 %add_add_fusion = f32[2048,512]{1,0:T(8,128)S(1)} fusion(f32[2048,512]{1,0:T(8,128)S(1)} %fusion.44, f32[2048,512]{1,0:T(8,128)S(1)} %fusion.46, bf16[2048,512]{1,0:T(8,128)(2,1)S(1)} %bitcast.124, f32[512]{0:T(512)S(1)} %copy-done.5, bf16[3,512,512]{2,1,0:T(8,128)(2,1)S(1)} %copy-done.2), kind=kOutput, calls=%fused_computation.4 | convolution fusion | flops 1076887552 | bytes 15206400 | tf_op jit(solution)/shard_map/dot_general | solution.py:79
  33.1 1.2 add_convert_fusion
  34.4 0.2 fusion.66
  34.6 4.6 %collective-permute-start.1 = (bf16[1,32,16,512]{3,2,1,0:T(8,128)(2,1)S(1)}, bf16[1,32,16,512]{3,2,1,0:T(8,128)(2,1)S(1)}, u32[]{:S(2)}, u32[]{:S(2)}) collective-permute-start(bf16[1,32,16,512]{3,2,1,0:T(8,128)(2,1)S(1)} %slice.136), channel_id=1, source_target_pairs={{0,2},{2,4},{4,6},{6,8},{8,10},{10,12},{12,14},{1,3},{3,5},{5,7},{... | collective-permute-start | bytes 1572872 | tf_op jit(solution)/shard_map/ppermute | solution.py:14
  39.2 0.7 fusion.39
  39.9 0.7 fusion.41
  40.6 8.8 %collective-permute-done.1 = bf16[1,32,16,512]{3,2,1,0:T(8,128)(2,1)S(1)} collective-permute-done((bf16[1,32,16,512]{3,2,1,0:T(8,128)(2,1)S(1)}, bf16[1,32,16,512]{3,2,1,0:T(8,128)(2,1)S(1)}, u32[]{:S(2)}, u32[]{:S(2)}) %collective-permute-start.1) | collective-permute-done | bytes 524320 | tf_op jit(solution)/shard_map/ppermute | solution.py:14
  49.5 0.2 pad_maximum_fusion
  49.8 0.6 copy-done.4
  50.4 0.8 add_convert_fusion.1
  51.2 0.2 fusion.68
  51.4 1.3 collective-permute-start.2
  52.7 1.5 %collective-permute-start.3 = (bf16[2,32,1,512]{3,2,1,0:T(2,128)(2,1)S(1)}, bf16[2,32,1,512]{3,2,1,0:T(2,128)(2,1)S(1)}, u32[]{:S(2)}, u32[]{:S(2)}) collective-permute-start(bf16[2,32,1,512]{3,2,1,0:T(2,128)(2,1)S(1)} %get-tuple-element.18), channel_id=1, source_target_pairs={{1,0},{3,2},{5,4},{7,6},{9,8},{11,10},{13,12},{15,14},{17,16},{19,... | collective-permute-start | bytes 196616 | tf_op jit(solution)/shard_map/ppermute | solution.py:25
  54.2 0.7 fusion.28
  54.9 1.0 collective-permute-done.3
  55.9 1.1 fusion.10
  57.0 1.0 fusion.67
  58.0 0.7 fusion.22
  58.7 0.7 fusion.24
  59.4 0.7 fusion.32
  60.1 0.7 fusion.34
  60.8 0.7 fusion.36
  61.5 1.0 pad_maximum_fusion.2
  62.5 0.7 fusion.26
  63.3 0.7 fusion.30
  64.0 1.6 %add_add_fusion.1 = f32[1024,512]{1,0:T(8,128)S(1)} fusion(f32[1024,512]{1,0:T(8,128)S(1)} %fusion.22, f32[1024,512]{1,0:T(8,128)S(1)} %fusion.24, f32[1024,512]{1,0:T(8,128)S(1)} %fusion.26, f32[1024,512]{1,0:T(8,128)S(1)} %fusion.28, f32[1024,512]{1,0:T(8,128)S(1)} %fusion.30, f32[1024,512]{1,0:T(8,128)S(1)} %fusion.32, f32[1024,512]{1,0:T(8,128)S(1)} %fusion.34, ...), kind=kOutput, calls=%fused_computation.16 | convolution fusion | flops 541589504 | bytes 20449280 | tf_op jit(solution)/shard_map/dot_general | solution.py:109
  65.6 1.7 %fusion.5 = bf16[2,8,64,512]{3,2,0,1:T(8,128)(2,1)} fusion(f32[2,8,64,512]{3,2,1,0:T(8,128)S(1)} %bitcast.125, bf16[2,8,64,512]{3,2,1,0:T(8,128)(2,1)S(1)} %bitcast.121), kind=kLoop, calls=%fused_computation.14 | loop fusion | flops 3670016 | bytes 4194304 | tf_op jit(solution)/shard_map/convert_element_type | solution.py:116
  67.3 7.8 %all-to-all-start = ((bf16[2,8,64,512]{3,2,0,1:T(8,128)(2,1)}), bf16[2,8,64,512]{3,2,0,1:T(8,128)(2,1)S(1)}, u32[]{:S(2)}, u32[]{:S(2)}) async-start(bf16[2,8,64,512]{3,2,0,1:T(8,128)(2,1)} %fusion.5), calls=%async_computation | async-start | bytes 2097152 | tf_op jit(solution)/shard_map/all_to_all | solution.py:124
  75.1 26.1 %all-to-all-done = bf16[2,8,64,512]{3,2,0,1:T(8,128)(2,1)S(1)} async-done(((bf16[2,8,64,512]{3,2,0,1:T(8,128)(2,1)}), bf16[2,8,64,512]{3,2,0,1:T(8,128)(2,1)S(1)}, u32[]{:S(2)}, u32[]{:S(2)}) %all-to-all-start) | async-done | bytes 1048608 | tf_op jit(solution)/shard_map/all_to_all | solution.py:124
  101.2 0.3 multiply_reduce_fusion
  101.6 0.3 fusion.3
  101.9 0.7 convolution_convert_fusion.1
  102.6 0.7 convolution_convert_fusion
  103.3 1.3 fusion.13
  104.6 0.2 fusion.69
  104.8 0.7 convolution_convert_fusion.2
  105.5 3.1 %fusion.16 = bf16[64,512,16]{1,2,0:T(8,128)(2,1)} fusion(bf16[16,64,512]{2,1,0:T(8,128)(2,1)S(1)} %bitcast.140, f32[64,16]{1,0:T(8,128)S(1)} %fusion.69, f32[64,16,16]{1,2,0:T(8,128)} %copy-done.11), kind=kOutput, calls=%fused_computation.33 | convolution fusion | flops 16827408 | bytes 2166784 | tf_op jit(solution)/shard_map/pst,tpc->spc/dot_general | solution.py:59
  108.6 2.1 %fusion.4 = bf16[16,64,512]{2,1,0:T(8,128)(2,1)S(1)} fusion(bf16[64,512,16]{1,2,0:T(8,128)(2,1)} %fusion.16, bf16[512,512]{1,0:T(8,128)(2,1)S(1)} %copy-done.10, bf16[2,8,64,512]{3,2,0,1:T(8,128)(2,1)S(1)} %all-to-all-done), kind=kOutput, calls=%fused_computation.11 | convolution fusion | flops 538443776 | bytes 3670016 | tf_op jit(solution)/shard_map/dot_general | solution.py:62
  110.7 29.3 %all_to_all.24 = bf16[16,64,512]{2,1,0:T(8,128)(2,1)S(1)} all-to-all(bf16[16,64,512]{2,1,0:T(8,128)(2,1)S(1)} %fusion.4), channel_id=1, replica_groups=mesh['clips'=2,'tm'=8,'cols'=2] {'tm'}, dimensions={0} | all-to-all | bytes 2097152 | tf_op jit(solution)/shard_map/all_to_all | solution.py:126
  140.0 1.1 copy.22
  (34 shorter events, 0.4 us)
Async XLA Ops:
  0.0 101.9 %copy-start = (bf16[512,512]{1,0:T(8,128)(2,1)S(1)}, bf16[512,512]{1,0:T(8,128)(2,1)}, u32[]{:S(2)}) copy-start(bf16[512,512]{1,0:T(8,128)(2,1)} %param.20) | copy-start | bytes 1572868
  0.0 6.4 %copy-start.1 = (bf16[4,32,16,512]{3,2,1,0:T(8,128)(2,1)S(1)}, bf16[4,32,16,512]{3,2,1,0:T(8,128)(2,1)}, u32[]{:S(2)}) copy-start(bf16[4,32,16,512]{3,2,1,0:T(8,128)(2,1)} %param.12) | copy-start | bytes 6291460
  1.5 27.3 %collective-permute-start = (bf16[2,32,16,512]{3,2,1,0:T(8,128)(2,1)S(1)}, bf16[2,32,16,512]{3,2,1,0:T(8,128)(2,1)S(1)}, u32[]{:S(2)}, u32[]{:S(2)}) collective-permute-start(bf16[2,32,16,512]{3,2,1,0:T(8,128)(2,1)S(1)} %slice.103), channel_id=1, source_target_pairs={{0,2},{2,4},{4,6},{6,8},{8,10},{10,12},{12,14},{1,3},{3,5},{5,7},{... | collective-permute-start | bytes 3145736 | tf_op jit(solution)/shard_map/ppermute | solution.py:14
  29.0 1.4 %copy-start.2 = (bf16[3,512,512]{2,1,0:T(8,128)(2,1)S(1)}, bf16[3,512,512]{2,1,0:T(8,128)(2,1)}, u32[]{:S(2)}) copy-start(bf16[3,512,512]{2,1,0:T(8,128)(2,1)} %param.13) | copy-start | bytes 4718596
  30.4 1.3 copy-start.5
  34.4 4.8 %copy-start.3 = (bf16[3,512,512]{2,1,0:T(8,128)(2,1)S(1)}, bf16[3,512,512]{2,1,0:T(8,128)(2,1)}, u32[]{:S(2)}) copy-start(bf16[3,512,512]{2,1,0:T(8,128)(2,1)} %param.15) | copy-start | bytes 4718596
  34.6 14.8 %collective-permute-start.1 = (bf16[1,32,16,512]{3,2,1,0:T(8,128)(2,1)S(1)}, bf16[1,32,16,512]{3,2,1,0:T(8,128)(2,1)S(1)}, u32[]{:S(2)}, u32[]{:S(2)}) collective-permute-start(bf16[1,32,16,512]{3,2,1,0:T(8,128)(2,1)S(1)} %slice.136), channel_id=1, source_target_pairs={{0,2},{2,4},{4,6},{6,8},{8,10},{10,12},{12,14},{1,3},{3,5},{5,7},{... | collective-permute-start | bytes 1572872 | tf_op jit(solution)/shard_map/ppermute | solution.py:14
  39.9 14.2 %slice-start = ((s8[4718592]{0:T(1024)(128)(4,1)}), s8[4194304]{0:T(1024)(128)(4,1)S(1)}, s32[]{:S(2)}) async-start(s8[4718592]{0:T(1024)(128)(4,1)} %bitcast.126), calls=%async_computation.2 | async-start | bytes 8388608
  49.7 0.7 copy-start.4
  49.7 4.5 %slice-start.1 = ((s8[4718592]{0:T(1024)(128)(4,1)}), s8[524288]{0:T(1024)(128)(4,1)S(1)}, s32[]{:S(2)}) async-start(s8[4718592]{0:T(1024)(128)(4,1)} %bitcast.126), calls=%async_computation.3 | async-start | bytes 1048576
  51.4 3.5 %collective-permute-start.2 = (bf16[2,32,1,512]{3,2,1,0:T(2,128)(2,1)S(1)}, bf16[2,32,1,512]{3,2,1,0:T(2,128)(2,1)S(1)}, u32[]{:S(2)}, u32[]{:S(2)}) collective-permute-start(bf16[2,32,1,512]{3,2,1,0:T(2,128)(2,1)S(1)} %get-tuple-element.17), channel_id=1, source_target_pairs={{0,1},{2,3},{4,5},{6,7},{8,9},{10,11},{12,13},{14,15},{16,17},{18,... | collective-permute-start | bytes 196616 | tf_op jit(solution)/shard_map/ppermute | solution.py:24
  52.7 3.2 %collective-permute-start.3 = (bf16[2,32,1,512]{3,2,1,0:T(2,128)(2,1)S(1)}, bf16[2,32,1,512]{3,2,1,0:T(2,128)(2,1)S(1)}, u32[]{:S(2)}, u32[]{:S(2)}) collective-permute-start(bf16[2,32,1,512]{3,2,1,0:T(2,128)(2,1)S(1)} %get-tuple-element.18), channel_id=1, source_target_pairs={{1,0},{3,2},{5,4},{7,6},{9,8},{11,10},{13,12},{15,14},{17,16},{19,... | collective-permute-start | bytes 196616 | tf_op jit(solution)/shard_map/ppermute | solution.py:25
  63.2 0.7 copy-start.7
  67.3 34.2 %copy-start.6 = (f32[512]{0:T(512)S(1)}, f32[512]{0:T(512)}, u32[]{:S(2)}) copy-start(f32[512]{0:T(512)} %param.19) | copy-start | bytes 6148
  67.3 33.9 %all-to-all-start = ((bf16[2,8,64,512]{3,2,0,1:T(8,128)(2,1)}), bf16[2,8,64,512]{3,2,0,1:T(8,128)(2,1)S(1)}, u32[]{:S(2)}, u32[]{:S(2)}) async-start(bf16[2,8,64,512]{3,2,0,1:T(8,128)(2,1)} %fusion.5), calls=%async_computation | async-start | bytes 2097152 | tf_op jit(solution)/shard_map/all_to_all | solution.py:124
  101.6 1.0 copy-start.8
  103.3 1.5 %copy-start.9 = (bf16[512,512]{1,0:T(8,128)(2,1)S(1)}, bf16[512,512]{1,0:T(8,128)(2,1)}, u32[]{:S(2)}) copy-start(bf16[512,512]{1,0:T(8,128)(2,1)} %param.22) | copy-start | bytes 1572868
  104.6 0.9 copy-start.11
  105.5 3.1 %copy-start.10 = (bf16[512,512]{1,0:T(8,128)(2,1)S(1)}, bf16[512,512]{1,0:T(8,128)(2,1)}, u32[]{:S(2)}) copy-start(bf16[512,512]{1,0:T(8,128)(2,1)} %param.23) | copy-start | bytes 1572868
where the time goes:
time: 142 us; the launch traced here: 141 us
  waiting for transfers between devices  56 us (39%)
  blocking collectives  29.3 us (21%)
  matrix products  22.9 us (16%)
  starting transfers between devices  20.1 us (14%)
  local copies, waits for them, and re-layouts  6.39 us (4%)
  other arithmetic  6.07 us (4%)
    all_to_all x1, blocking collectives, per_device(): lax.all_to_all(attended, 'tm', split_axis=0, concat_axis=1, tiled=True)  29.3 us
    ppermute x2, waiting for transfers between devices, passed_along(): lax.ppermute(value, axis, [(source, source + steps) for source in range(f...  28.9 us
    all_to_all x1, waiting for transfers between devices, per_device(): lax.all_to_all(grouped, 'tm', split_axis=1, concat_axis=0, tiled=True)  26.1 us
    ppermute x2, starting transfers between devices, passed_along(): lax.ppermute(value, axis, [(source, source + steps) for source in range(f...  9.52 us
    all_to_all x1, starting transfers between devices, per_device(): lax.all_to_all(grouped, 'tm', split_axis=1, concat_axis=0, tiled=True)  7.78 us
    dot_general x9, matrix products, per_device(): jnp.dot(window.reshape(-1, channels), w_space[3 * row_tap + col_tap], pre...  7.23 us
    dot_general x3, matrix products, temporal(): jnp.dot(window.reshape(-1, channels), weights[offset], preferred_element_...  4.99 us
    dot_general x1, matrix products, attend(): jnp.einsum('pst,tpc->spc', probs, value, preferred_element_type=jnp.float32)  3.05 us
  transfers between devices with their start and end apart: 5, of which 4 were waited for; matrix products, arithmetic and copies ran while one was open for 3% of the time, Pallas kernels for 0%

commit v1 on v0

v1 whole, which is shorter than its diff:
```python
from functools import partial

import jax
import jax.numpy as jnp
from jax import lax
from jax.experimental import pallas as pl
from jax.experimental.pallas import tpu as pltpu
from jax.sharding import PartitionSpec as P

epsilon = 1e-06
MESH = pl.DeviceIdType.MESH


def passed_along(value, axis, steps):
    count = lax.axis_size(axis)
    first, last = (max(0, -steps), min(count, count - steps))
    return lax.ppermute(value, axis, [(source, source + steps) for source in range(first, last)])


def padded(x, sides, width):
    for axis, dim in sides:
        devices, length = (lax.axis_size(axis), x.shape[dim])
        up = [(i, (i + 1) % devices) for i in range(devices - 1)]
        down = [(j, i) for i, j in up]
        last = lax.slice_in_dim(x, length - width, length, axis=dim)
        first = lax.slice_in_dim(x, 0, width, axis=dim)
        before = lax.ppermute(last, axis, up)
        after = lax.ppermute(first, axis, down)
        x = jnp.concatenate([before, x, after], axis=dim)
    return x


def attention_kernel(
    x_ref, gain_ref, wq_ref, wk_ref, wv_ref, wo_ref, y_ref,
    held, done, send_sem, recv_sem, back_sem, home_sem,
):
    halves, owners, chunks, pixels, channels = x_ref.shape
    frames = owners * halves
    rows = frames * pixels
    me = lax.axis_index("tm")

    barrier = pltpu.get_barrier_semaphore()

    def greet(k, _):
        peer = lax.rem(me + k, owners)
        pl.semaphore_signal(barrier, inc=1, device_id={"tm": peer}, device_id_type=MESH)
        return 0

    lax.fori_loop(1, owners, greet, 0)
    pl.semaphore_wait(barrier, owners - 1)

    def outward(c, peer, slot, source):
        return pltpu.make_async_remote_copy(
            src_ref=x_ref.at[:, peer, c],
            dst_ref=held.at[c, source],
            send_sem=send_sem.at[c, slot],
            recv_sem=recv_sem.at[c, source],
            device_id={"tm": peer},
            device_id_type=MESH,
        )

    def homeward(c, peer, slot, source):
        return pltpu.make_async_remote_copy(
            src_ref=done.at[c, peer],
            dst_ref=y_ref.at[:, source, c],
            send_sem=back_sem.at[c, slot],
            recv_sem=home_sem.at[c, source],
            device_id={"tm": peer},
            device_id_type=MESH,
        )

    for c in range(chunks):
        def send(k, _):
            outward(c, lax.rem(me + k, owners), k, me).start()
            return 0

        lax.fori_loop(1, owners, send, 0)

    place = lax.broadcasted_iota(jnp.int32, (rows, rows), 0)
    other = lax.broadcasted_iota(jnp.int32, (rows, rows), 1)
    allowed = (lax.rem(place, pixels) == lax.rem(other, pixels)) & (other <= place)

    for c in range(chunks):
        held[c, me] = x_ref[:, me, c]

        def arrive(k, _):
            source = lax.rem(me + owners - k, owners)
            outward(c, lax.rem(me + k, owners), k, source).wait_recv()
            return 0

        lax.fori_loop(1, owners, arrive, 0)
        wide = held[c].reshape(rows, channels).astype(jnp.float32)
        scale = lax.rsqrt(jnp.mean(wide * wide, axis=-1, keepdims=True) + epsilon)
        normed = (wide * scale * gain_ref[...]).astype(jnp.bfloat16)
        query = jnp.dot(normed, wq_ref[...], preferred_element_type=jnp.float32).astype(jnp.bfloat16)
        key = jnp.dot(normed, wk_ref[...], preferred_element_type=jnp.float32).astype(jnp.bfloat16)
        value = jnp.dot(normed, wv_ref[...], preferred_element_type=jnp.float32).astype(jnp.bfloat16)
        scores = lax.dot_general(
            query, key, (((1,), (1,)), ((), ())), preferred_element_type=jnp.float32
        ) * channels ** (-0.5)
        scores = jnp.where(allowed, scores, -1e30)
        largest = jnp.max(scores, axis=-1, keepdims=True)
        probs = jnp.exp(scores - largest)
        probs = (probs / jnp.sum(probs, axis=-1, keepdims=True)).astype(jnp.bfloat16)
        context = jnp.dot(probs, value, preferred_element_type=jnp.float32).astype(jnp.bfloat16)
        mixed = jnp.dot(context, wo_ref[...], preferred_element_type=jnp.float32)
        result = (wide + mixed).astype(jnp.bfloat16)
        done[c] = result.reshape(owners, halves, pixels, channels)

        def back(k, _):
            homeward(c, lax.rem(me + k, owners), k, me).start()
            return 0

        lax.fori_loop(1, owners, back, 0)
        y_ref[:, me, c] = done[c, me]

    for c in range(chunks):
        def finish(k, _):
            peer, source = lax.rem(me + k, owners), lax.rem(me + owners - k, owners)
            outward(c, peer, k, me).wait_send()
            homeward(c, peer, k, me).wait_send()
            homeward(c, peer, k, source).wait_recv()
            return 0

        lax.fori_loop(1, owners, finish, 0)


def attend(spatial, gain, w_query, w_key, w_value, w_out):
    halves, height, strip, channels = spatial.shape
    owners = lax.axis_size("tm")
    owned = height * strip // owners
    pixels = min(16, owned)
    chunks = owned // pixels
    vmem = pl.BlockSpec(memory_space=pltpu.VMEM)
    result = pl.pallas_call(
        attention_kernel,
        out_shape=jax.ShapeDtypeStruct((halves, owners, chunks, pixels, channels), jnp.bfloat16),
        in_specs=[vmem] * 6,
        out_specs=vmem,
        scratch_shapes=[
            pltpu.VMEM((chunks, owners, halves, pixels, channels), jnp.bfloat16),
            pltpu.VMEM((chunks, owners, halves, pixels, channels), jnp.bfloat16),
            pltpu.SemaphoreType.DMA((chunks, owners)),
            pltpu.SemaphoreType.DMA((chunks, owners)),
            pltpu.SemaphoreType.DMA((chunks, owners)),
            pltpu.SemaphoreType.DMA((chunks, owners)),
        ],
        compiler_params=pltpu.CompilerParams(
            collective_id=0, has_side_effects=True, vmem_limit_bytes=48 * 1024 * 1024
        ),
    )(
        spatial.reshape(halves, owners, chunks, pixels, channels),
        gain.reshape(1, channels), w_query, w_key, w_value, w_out,
    )
    return result.reshape(halves, height, strip, channels)


def temporal(extended, weights, bias, first, count):
    _, height, strip, channels = extended.shape
    summed = jnp.zeros((count * height * strip, channels), jnp.float32) + bias
    for offset in range(3):
        window = extended[first - offset : first - offset + count]
        summed = summed + jnp.dot(
            window.reshape(-1, channels), weights[offset], preferred_element_type=jnp.float32
        )
    return summed.reshape(count, height, strip, channels)


def lift(extended, weights, bias, first, count):
    summed = temporal(extended, weights, bias, first, count)
    return (extended[first : first + count].astype(jnp.float32) + jax.nn.silu(summed)).astype(jnp.bfloat16)


def per_device(
    video, w_time, b_time, w_down, b_down, w_space, b_space, gain, w_query, w_key, w_value, w_out
):
    frames, height, strip, channels = video.shape
    late = lift(video, w_time, b_time, 2, frames - 2)
    before = passed_along(video[frames - 2 :], "tm", 1)
    carried = passed_along(late[-1:], "tm", 1)
    extended = jnp.concatenate([before, video[:2]], 0)
    early = lift(extended, w_time, b_time, 2, 2)
    lifted_ext = jnp.concatenate([carried, early, late], 0)
    halves = frames // 2
    taps = [lifted_ext[2 : frames + 1 : 2], lifted_ext[1:frames:2], lifted_ext[0 : frames - 1 : 2]]
    summed = jnp.zeros((halves * height * strip, channels), jnp.float32) + b_down
    for offset in range(3):
        summed = summed + jnp.dot(
            taps[offset].reshape(-1, channels), w_down[offset], preferred_element_type=jnp.float32
        )
    reduced = summed.reshape(halves, height, strip, channels).astype(jnp.bfloat16)
    framed = padded(reduced, (("cols", 2),), 1)
    framed = jnp.pad(framed, ((0, 0), (1, 1), (0, 0), (0, 0)))
    summed = jnp.zeros((halves * height * strip, channels), jnp.float32) + b_space
    for row_tap in range(3):
        for col_tap in range(3):
            window = framed[:, row_tap : row_tap + height, col_tap : col_tap + strip]
            summed = summed + jnp.dot(
                window.reshape(-1, channels),
                w_space[3 * row_tap + col_tap],
                preferred_element_type=jnp.float32,
            )
    spatial = (
        reduced.astype(jnp.float32) + jax.nn.silu(summed.reshape(halves, height, strip, channels))
    ).astype(jnp.bfloat16)
    return attend(spatial, gain, w_query, w_key, w_value, w_out)


def solution(mesh):
    return jax.shard_map(
        per_device,
        mesh=mesh,
        in_specs=(P(("clips", "tm"), None, "cols", None),) + (P(),) * 11,
        out_specs=P(("clips", "tm"), None, "cols", None),
        check_vma=False,
    )
```

time: 142 us -> 122 us (0.86)
  Pallas kernels: 0 us -> 52.7 us
  blocking collectives: 29.3 us -> 0 us
  waiting for transfers between devices: 56 us -> 30.8 us
  matrix products: 22.9 us -> 13.6 us
  starting transfers between devices: 20.1 us -> 12.2 us
  other arithmetic: 6.07 us -> 4.26 us
    pallas_call x0 -> x1, Pallas kernels: none -> 52.7 us  [attend(): pl.pallas_call(attention_kernel, out_shape=jax.ShapeDtypeStruct((halves,...]
    all_to_all x1 -> x0, blocking collectives: 29.3 us -> none  [per_device(): lax.all_to_all(attended, 'tm', split_axis=0, concat_axis=1, tiled=True)]
    all_to_all x1 -> x0, waiting for transfers between devices: 26.1 us -> none  [per_device(): lax.all_to_all(grouped, 'tm', split_axis=1, concat_axis=0, tiled=True)]
    dot_general x6 -> x0, matrix products: 8.51 us -> none  [the longest x1 3.05 us: attend(): jnp.einsum('pst,tpc->spc', probs, value, preferred_element_type=jnp.float32)]
    all_to_all x1 -> x0, starting transfers between devices: 7.78 us -> none  [per_device(): lax.all_to_all(grouped, 'tm', split_axis=1, concat_axis=0, tiled=True)]
    unnamed x29 -> x27, local copies, waits for them, and re-layouts: 1.5 us -> 3.71 us
    slice x1, local copies, waits for them, and re-layouts: 0.62 us -> 2.3 us  [temporal(): window = extended[first - offset:first - offset + count]]
    slice x3 -> x1, local copies, waits for them, and re-layouts: 1.66 us -> 0.04 us  [per_device(): carried = passed_along(late[-1:], 'tm', 1)]
  transfers between devices with their start and end apart: 5 -> 4, of which waited for: 4 -> 3; matrix products, arithmetic and copies ran while one was open for 3% -> 3% of each run, Pallas kernels for 0% -> 0%
where the time goes in v1:
time: 122 us; the launch traced here: 121 us
  Pallas kernels  52.7 us (43%)
  waiting for transfers between devices  30.8 us (25%)
  matrix products  13.6 us (11%)
  starting transfers between devices  12.2 us (10%)
  local copies, waits for them, and re-layouts  7.52 us (6%)
  other arithmetic  4.26 us (3%)
    pallas_call x1, Pallas kernels, attend(): pl.pallas_call(attention_kernel, out_shape=jax.ShapeDtypeStruct((halves,...  52.7 us
    ppermute x2, waiting for transfers between devices, passed_along(): lax.ppermute(value, axis, [(source, source + steps) for source in range(f...  29.8 us
    ppermute x2, starting transfers between devices, passed_along(): lax.ppermute(value, axis, [(source, source + steps) for source in range(f...  9.38 us
    dot_general x9, matrix products, per_device(): jnp.dot(window.reshape(-1, channels), w_space[3 * row_tap + col_tap], pre...  7.26 us
    dot_general x6, matrix products, temporal(): jnp.dot(window.reshape(-1, channels), weights[offset], preferred_element_...  4.25 us
    unnamed x27, local copies, waits for them, and re-layouts  3.71 us
  transfers between devices with their start and end apart: 4, of which 3 were waited for; matrix products, arithmetic and copies ran while one was open for 3% of the time, Pallas kernels for 0%

profile of v1, /device:TPU:0, one launch (start us, length us, event | category | flops | bytes accessed | tf_op | source)
XLA Modules:
  0.0 121.4 jit_solution(17223355020777413802)
XLA Ops:
  0.0 2.3 %fusion.61 = (bf16[2,32,16,512]{3,2,1,0:T(8,128)(2,1)S(1)}, bf16[2,32,16,512]{3,2,1,0:T(8,128)(2,1)S(1)}, bf16[2,32,16,512]{3,2,1,0:T(8,128)(2,1)S(1)}) fusion(bf16[4,32,16,512]{3,2,1,0:T(8,128)(2,1)} %param.12), kind=kLoop, calls=%fused_computation.72 | loop fusion | bytes 6291456 | tf_op jit(solution)/shard_map/slice | solution.py:162
  2.3 5.0 %collective-permute-start.1 = (bf16[2,32,16,512]{3,2,1,0:T(8,128)(2,1)S(1)}, bf16[2,32,16,512]{3,2,1,0:T(8,128)(2,1)S(1)}, u32[]{:S(2)}, u32[]{:S(2)}) collective-permute-start(bf16[2,32,16,512]{3,2,1,0:T(8,128)(2,1)S(1)} %get-tuple-element.11), channel_id=1, source_target_pairs={{0,2},{2,4},{4,6},{6,8},{8,10},{10,12},{12,14},{1,3},{3,5},{5,7},{... | collective-permute-start | bytes 3145736 | tf_op jit(solution)/shard_map/ppermute | solution.py:17
  7.3 0.7 fusion.38
  8.0 0.7 fusion.40
  8.7 0.7 fusion.36
  9.4 0.7 add_add_fusion.2
  10.1 19.5 %collective-permute-done.1 = bf16[2,32,16,512]{3,2,1,0:T(8,128)(2,1)S(1)} collective-permute-done((bf16[2,32,16,512]{3,2,1,0:T(8,128)(2,1)S(1)}, bf16[2,32,16,512]{3,2,1,0:T(8,128)(2,1)S(1)}, u32[]{:S(2)}, u32[]{:S(2)}) %collective-permute-start.1) | collective-permute-done | bytes 1048608 | tf_op jit(solution)/shard_map/ppermute | solution.py:17
  29.6 0.1 pad_maximum_fusion.3
  29.7 0.7 fusion.34
  30.4 0.0 copy-start.5
  30.4 0.7 add_add_fusion.1
  31.2 0.8 copy-done.5
  32.0 1.2 add_convert_fusion.1
  33.2 4.4 %collective-permute-start = (bf16[1,32,16,512]{3,2,1,0:T(8,128)(2,1)S(1)}, bf16[1,32,16,512]{3,2,1,0:T(8,128)(2,1)S(1)}, u32[]{:S(2)}, u32[]{:S(2)}) collective-permute-start(bf16[1,32,16,512]{3,2,1,0:T(8,128)(2,1)S(1)} %slice.144), channel_id=1, source_target_pairs={{0,2},{2,4},{4,6},{6,8},{8,10},{10,12},{12,14},{1,3},{3,5},{5,7},{... | collective-permute-start | bytes 1572872 | tf_op jit(solution)/shard_map/ppermute | solution.py:17
  37.7 10.3 %collective-permute-done = bf16[1,32,16,512]{3,2,1,0:T(8,128)(2,1)S(1)} collective-permute-done((bf16[1,32,16,512]{3,2,1,0:T(8,128)(2,1)S(1)}, bf16[1,32,16,512]{3,2,1,0:T(8,128)(2,1)S(1)}, u32[]{:S(2)}, u32[]{:S(2)}) %collective-permute-start) | collective-permute-done | bytes 524320 | tf_op jit(solution)/shard_map/ppermute | solution.py:17
  48.0 0.3 pad_maximum_fusion
  48.2 0.0 slice-start
  48.3 0.4 fusion.60
  48.6 1.0 copy-done.7
  49.6 0.7 fusion.25
  50.4 0.0 slice-start.1
  50.4 0.7 fusion.27
  51.1 0.7 add_convert_fusion
  51.8 0.2 fusion.63
  52.0 1.3 %collective-permute-start.2 = (bf16[2,32,1,512]{3,2,1,0:T(2,128)(2,1)S(1)}, bf16[2,32,1,512]{3,2,1,0:T(2,128)(2,1)S(1)}, u32[]{:S(2)}, u32[]{:S(2)}) collective-permute-start(bf16[2,32,1,512]{3,2,1,0:T(2,128)(2,1)S(1)} %get-tuple-element.21), channel_id=1, source_target_pairs={{0,1},{2,3},{4,5},{6,7},{8,9},{10,11},{12,13},{14,15},{16,17},{18,... | collective-permute-start | bytes 196616 | tf_op jit(solution)/shard_map/ppermute | solution.py:27
  53.3 1.5 %collective-permute-start.3 = (bf16[2,32,1,512]{3,2,1,0:T(2,128)(2,1)S(1)}, bf16[2,32,1,512]{3,2,1,0:T(2,128)(2,1)S(1)}, u32[]{:S(2)}, u32[]{:S(2)}) collective-permute-start(bf16[2,32,1,512]{3,2,1,0:T(2,128)(2,1)S(1)} %get-tuple-element.22), channel_id=1, source_target_pairs={{1,0},{3,2},{5,4},{7,6},{9,8},{11,10},{13,12},{15,14},{17,16},{19,... | collective-permute-start | bytes 196616 | tf_op jit(solution)/shard_map/ppermute | solution.py:28
  54.8 0.7 fusion.14
  55.6 1.0 collective-permute-done.3
  56.6 1.0 pad_maximum_fusion.2
  57.6 0.7 fusion.12
  58.3 0.7 fusion.16
  59.0 1.1 fusion.6
  60.1 0.9 fusion.62
  61.0 0.7 fusion.10
  61.7 0.7 fusion.18
  62.4 0.7 fusion.20
  63.1 0.7 fusion.22
  63.8 0.0 copy-start.10
  63.8 0.7 fusion.8
  64.5 1.6 %add_add_fusion = f32[1024,512]{1,0:T(8,128)S(1)} fusion(f32[1024,512]{1,0:T(8,128)S(1)} %fusion.8, f32[1024,512]{1,0:T(8,128)S(1)} %fusion.10, f32[1024,512]{1,0:T(8,128)S(1)} %fusion.12, f32[1024,512]{1,0:T(8,128)S(1)} %fusion.14, f32[1024,512]{1,0:T(8,128)S(1)} %fusion.16, f32[1024,512]{1,0:T(8,128)S(1)} %fusion.18, f32[1024,512]{1,0:T(8,128)S(1)} %fusion.20, ...), kind=kOutput, calls=%fused_computation.6 | convolution fusion | flops 541589504 | bytes 20449280 | tf_op jit(solution)/shard_map/dot_general | solution.py:198
  66.2 0.0 copy-start.1
  66.2 0.7 fusion.1.x_ref
  66.9 0.3 copy-done
  67.2 0.2 copy-done.1
  67.4 0.2 copy-done.2
  67.6 0.2 copy-done.3
  67.7 52.7 %shard_map.118 = bf16[2,8,4,16,512]{4,3,2,1,0:T(8,128)(2,1)S(1)} custom-call(bf16[2,8,4,16,512]{4,3,2,1,0:T(8,128)(2,1)S(1)} %fusion.1.x_ref, f32[1,512]{1,0:T(1,128)S(1)} %bitcast.96, bf16[512,512]{1,0:T(8,128)(2,1)S(1)} %copy-done, bf16[512,512]{1,0:T(8,128)(2,1)S(1)} %copy-done.1, bf16[512,512]{1,0:T(8,128)(2,1)S(1)} %copy-done.2, ...), custom_call_target="tpu_custom_call" | custom-call | tf_op jit(solution)/shard_map/pallas_call | solution.py:135
  120.4 1.0 copy.14
  (18 shorter events, 0.1 us)
Async XLA Ops:
  0.0 7.3 %copy-start.6 = (bf16[3,512,512]{2,1,0:T(8,128)(2,1)S(1)}, bf16[3,512,512]{2,1,0:T(8,128)(2,1)}, u32[]{:S(2)}) copy-start(bf16[3,512,512]{2,1,0:T(8,128)(2,1)} %param.13) | copy-start | bytes 4718596
  2.3 27.3 %collective-permute-start.1 = (bf16[2,32,16,512]{3,2,1,0:T(8,128)(2,1)S(1)}, bf16[2,32,16,512]{3,2,1,0:T(8,128)(2,1)S(1)}, u32[]{:S(2)}, u32[]{:S(2)}) collective-permute-start(bf16[2,32,16,512]{3,2,1,0:T(8,128)(2,1)S(1)} %get-tuple-element.11), channel_id=1, source_target_pairs={{0,2},{2,4},{4,6},{6,8},{8,10},{10,12},{12,14},{1,3},{3,5},{5,7},{... | collective-permute-start | bytes 3145736 | tf_op jit(solution)/shard_map/ppermute | solution.py:17
  8.7 0.7 copy-start.8
  30.4 1.6 %copy-start.5 = (bf16[4,32,16,512]{3,2,1,0:T(8,128)(2,1)S(1)}, bf16[4,32,16,512]{3,2,1,0:T(8,128)(2,1)}, u32[]{:S(2)}) copy-start(bf16[4,32,16,512]{3,2,1,0:T(8,128)(2,1)} %param.12) | copy-start | bytes 6291460
  33.2 14.7 %collective-permute-start = (bf16[1,32,16,512]{3,2,1,0:T(8,128)(2,1)S(1)}, bf16[1,32,16,512]{3,2,1,0:T(8,128)(2,1)S(1)}, u32[]{:S(2)}, u32[]{:S(2)}) collective-permute-start(bf16[1,32,16,512]{3,2,1,0:T(8,128)(2,1)S(1)} %slice.144), channel_id=1, source_target_pairs={{0,2},{2,4},{4,6},{6,8},{8,10},{10,12},{12,14},{1,3},{3,5},{5,7},{... | collective-permute-start | bytes 1572872 | tf_op jit(solution)/shard_map/ppermute | solution.py:17
  48.2 1.4 %copy-start.7 = (bf16[3,512,512]{2,1,0:T(8,128)(2,1)S(1)}, bf16[3,512,512]{2,1,0:T(8,128)(2,1)}, u32[]{:S(2)}) copy-start(bf16[3,512,512]{2,1,0:T(8,128)(2,1)} %param.15) | copy-start | bytes 4718596
  48.2 6.6 %slice-start = ((s8[4718592]{0:T(1024)(128)(4,1)}), s8[4194304]{0:T(1024)(128)(4,1)S(1)}, s32[]{:S(2)}) async-start(s8[4718592]{0:T(1024)(128)(4,1)} %bitcast.106), calls=%async_computation | async-start | bytes 8388608
  50.3 0.7 copy-start.9
  50.4 4.5 %slice-start.1 = ((s8[4718592]{0:T(1024)(128)(4,1)}), s8[524288]{0:T(1024)(128)(4,1)S(1)}, s32[]{:S(2)}) async-start(s8[4718592]{0:T(1024)(128)(4,1)} %bitcast.106), calls=%async_computation.1 | async-start | bytes 1048576
  52.0 3.5 %collective-permute-start.2 = (bf16[2,32,1,512]{3,2,1,0:T(2,128)(2,1)S(1)}, bf16[2,32,1,512]{3,2,1,0:T(2,128)(2,1)S(1)}, u32[]{:S(2)}, u32[]{:S(2)}) collective-permute-start(bf16[2,32,1,512]{3,2,1,0:T(2,128)(2,1)S(1)} %get-tuple-element.21), channel_id=1, source_target_pairs={{0,1},{2,3},{4,5},{6,7},{8,9},{10,11},{12,13},{14,15},{16,17},{18,... | collective-permute-start | bytes 196616 | tf_op jit(solution)/shard_map/ppermute | solution.py:27
  53.3 3.2 %collective-permute-start.3 = (bf16[2,32,1,512]{3,2,1,0:T(2,128)(2,1)S(1)}, bf16[2,32,1,512]{3,2,1,0:T(2,128)(2,1)S(1)}, u32[]{:S(2)}, u32[]{:S(2)}) collective-permute-start(bf16[2,32,1,512]{3,2,1,0:T(2,128)(2,1)S(1)} %get-tuple-element.22), channel_id=1, source_target_pairs={{1,0},{3,2},{5,4},{7,6},{9,8},{11,10},{13,12},{15,14},{17,16},{19,... | collective-permute-start | bytes 196616 | tf_op jit(solution)/shard_map/ppermute | solution.py:28
  63.8 0.7 copy-start.10
  66.2 1.0 copy-start
  66.2 1.2 copy-start.1
  66.2 1.3 %copy-start.2 = (bf16[512,512]{1,0:T(8,128)(2,1)S(1)}, bf16[512,512]{1,0:T(8,128)(2,1)}, u32[]{:S(2)}) copy-start(bf16[512,512]{1,0:T(8,128)(2,1)} %wv_ref.1) | copy-start | bytes 1572868
  66.2 1.5 %copy-start.3 = (bf16[512,512]{1,0:T(8,128)(2,1)S(1)}, bf16[512,512]{1,0:T(8,128)(2,1)}, u32[]{:S(2)}) copy-start(bf16[512,512]{1,0:T(8,128)(2,1)} %wo_ref.1) | copy-start | bytes 1572868
  66.2 1.5 %copy-start.4 = (f32[512]{0:T(512)S(1)}, f32[512]{0:T(512)}, u32[]{:S(2)}) copy-start(f32[512]{0:T(512)} %param.19) | copy-start | bytes 6148

commit v2 on v1

v2 whole, which is shorter than its diff:
```python
from functools import partial

import jax
import jax.numpy as jnp
from jax import lax
from jax.experimental import pallas as pl
from jax.experimental.pallas import tpu as pltpu
from jax.sharding import PartitionSpec as P

epsilon = 1e-06
MESH = pl.DeviceIdType.MESH


def block_kernel(
    shape, video, wt_hbm, bt, wd_hbm, bd, ws_hbm, bs, gain, wq_hbm, wk_hbm, wv_hbm, wo_hbm, y_ref,
    wt, wd, ws, wq, wk, wv, wo, before, carried, lifted, left_of, middle, right_of, partial_sum,
    edges, halo, spatial, held, done,
    load_sem, frame_send, frame_recv, edge_send, edge_recv, send_sem, recv_sem, back_sem, home_sem,
):
    height, strip = shape
    frames, area, channels = video.shape
    halves, owners, chunks, pixels, _ = y_ref.shape
    total = owners * halves
    rows = total * pixels
    me, col, cols = lax.axis_index("tm"), lax.axis_index("cols"), lax.axis_size("cols")
    f32, bf16 = jnp.float32, jnp.bfloat16
    tile = min(256, area)
    lines = tile // strip

    loads = [
        pltpu.make_async_copy(source, target, load_sem.at[i])
        for i, (source, target) in enumerate(
            ((wt_hbm, wt), (wd_hbm, wd), (ws_hbm, ws), (wq_hbm, wq), (wk_hbm, wk), (wv_hbm, wv), (wo_hbm, wo))
        )
    ]
    for load in loads:
        load.start()

    barrier = pltpu.get_barrier_semaphore()

    def greet(k, _):
        peer = lax.rem(me + k, owners)
        pl.semaphore_signal(barrier, inc=1, device_id={"tm": peer}, device_id_type=MESH)
        return 0

    lax.fori_loop(1, owners, greet, 0)

    def greet_side(k, _):
        peer = lax.rem(col + k, cols)
        pl.semaphore_signal(barrier, inc=1, device_id={"cols": peer}, device_id_type=MESH)
        return 0

    lax.fori_loop(1, cols, greet_side, 0)
    pl.semaphore_wait(barrier, owners + cols - 2)

    def onward(i):
        source, target = (
            (video.at[frames - 1], before.at[1]),
            (video.at[frames - 2], before.at[0]),
            (lifted.at[frames - 1], carried),
        )[i]
        return pltpu.make_async_remote_copy(
            src_ref=source, dst_ref=target, send_sem=frame_send.at[i], recv_sem=frame_recv.at[i],
            device_id={"tm": lax.rem(me + 1, owners)}, device_id_type=MESH,
        )

    has_next, has_before = me < owners - 1, me > 0

    def send_on(i):
        @pl.when(has_next)
        def _():
            onward(i).start()

    def take(i):
        target = (before.at[1], before.at[0], carried)[i]

        @pl.when(has_before)
        def _():
            onward(i).wait_recv()

        @pl.when(jnp.logical_not(has_before))
        def _():
            target[...] = jnp.zeros((area, channels), bf16)

    send_on(0)
    send_on(1)

    def frame_of(f):
        return video.at[f] if f >= 0 else before.at[f + 2]

    def lift(f):
        @pl.loop(0, area // tile)
        def _(t):
            part = pl.ds(pl.multiple_of(t * tile, tile), tile)
            summed = bt[...] + jnp.dot(frame_of(f)[part], wt[0], preferred_element_type=f32)
            summed = summed + jnp.dot(frame_of(f - 1)[part], wt[1], preferred_element_type=f32)
            summed = summed + jnp.dot(frame_of(f - 2)[part], wt[2], preferred_element_type=f32)
            lifted[f, part] = (video[f, part].astype(f32) + jax.nn.silu(summed)).astype(bf16)

    def sideways(s, side):
        peer = lax.rem(col + 1, cols) if side == 0 else lax.rem(col + cols - 1, cols)
        return pltpu.make_async_remote_copy(
            src_ref=edges.at[s, side], dst_ref=halo.at[s, side],
            send_sem=edge_send.at[s, side], recv_sem=edge_recv.at[s, side],
            device_id={"cols": peer}, device_id_type=MESH,
        )

    sends_side = (col < cols - 1, col > 0)
    takes_side = (col > 0, col < cols - 1)

    def reduce_frame(s):
        top = 2 * s + 1

        @pl.loop(0, area // tile)
        def _(t):
            part = pl.ds(pl.multiple_of(t * tile, tile), tile)
            oldest = carried[part] if s == 0 else lifted[top - 2, part]
            summed = bd[...] + jnp.dot(lifted[top, part], wd[0], preferred_element_type=f32)
            summed = summed + jnp.dot(lifted[top - 1, part], wd[1], preferred_element_type=f32)
            summed = summed + jnp.dot(oldest, wd[2], preferred_element_type=f32)
            reduced = summed.astype(bf16)
            middle[s, pl.ds(1 + t * lines, lines)] = reduced.reshape(lines, strip, channels)
            wide = reduced.astype(f32).reshape(lines, strip, channels)
            line = pl.ds(pl.multiple_of(t * lines, lines), lines)
            edges[s, 0, line] = wide[:, strip - 1].astype(bf16)
            edges[s, 1, line] = wide[:, 0].astype(bf16)

        for side in range(2):
            @pl.when(sends_side[side])
            def _():
                sideways(s, side).start()

    def convolve(s):
        for shifted in (left_of, middle, right_of):
            shifted[s, 0] = jnp.zeros((strip, channels), bf16)
            shifted[s, height + 1] = jnp.zeros((strip, channels), bf16)

        def taps(shifted, t, b, summed):
            for a in range(3):
                window = shifted[s, pl.ds(t * lines + a, lines)].reshape(tile, channels)
                summed = summed + jnp.dot(window, ws[3 * a + b], preferred_element_type=f32)
            return summed

        @pl.loop(0, area // tile)
        def _(t):
            part = pl.ds(pl.multiple_of(t * tile, tile), tile)
            partial_sum[part] = taps(middle, t, 1, jnp.zeros((tile, channels), f32) + bs[...])

        for side in range(2):
            @pl.when(takes_side[side])
            def _():
                sideways(s, side).wait_recv()

            @pl.when(jnp.logical_not(takes_side[side]))
            def _():
                halo[s, side] = jnp.zeros((height, channels), bf16)

        @pl.loop(0, area // tile)
        def _(t):
            line = pl.ds(pl.multiple_of(t * lines, lines), lines)
            wide = middle[s, pl.ds(1 + t * lines, lines)].astype(f32).reshape(tile, channels)
            place = lax.rem(lax.broadcasted_iota(jnp.int32, (tile, channels), 0), strip)

            def spread(side):
                column = halo[s, side, line].astype(f32)
                return jnp.broadcast_to(column[:, None, :], (lines, strip, channels)).reshape(tile, channels)

            lower = jnp.where(place == 0, spread(0), pltpu.roll(wide, 1, 0))
            upper = jnp.where(place == strip - 1, spread(1), pltpu.roll(wide, tile - 1, 0))
            left_of[s, pl.ds(1 + t * lines, lines)] = lower.astype(bf16).reshape(lines, strip, channels)
            right_of[s, pl.ds(1 + t * lines, lines)] = upper.astype(bf16).reshape(lines, strip, channels)

        groups = tile // pixels

        @pl.loop(0, area // tile)
        def _(t):
            part = pl.ds(pl.multiple_of(t * tile, tile), tile)
            summed = taps(left_of, t, 0, partial_sum[part])
            summed = taps(right_of, t, 2, summed)
            wide = middle[s, pl.ds(1 + t * lines, lines)].astype(f32).reshape(tile, channels)
            result = (wide + jax.nn.silu(summed)).astype(bf16)
            spatial[s, pl.ds(t * groups, groups)] = result.reshape(groups, pixels, channels)

    def outward(s, c, peer, slot, source):
        return pltpu.make_async_remote_copy(
            src_ref=spatial.at[s, peer * chunks + c],
            dst_ref=held.at[c, source, s],
            send_sem=send_sem.at[s, c, slot],
            recv_sem=recv_sem.at[s, c, source],
            device_id={"tm": peer},
            device_id_type=MESH,
        )

    def homeward(c, peer, slot, source):
        return pltpu.make_async_remote_copy(
            src_ref=done.at[c, peer],
            dst_ref=y_ref.at[:, source, c],
            send_sem=back_sem.at[c, slot],
            recv_sem=home_sem.at[c, source],
            device_id={"tm": peer},
            device_id_type=MESH,
        )

    def scatter(s):
        for c in range(chunks):
            def send(k, _):
                outward(s, c, lax.rem(me + k, owners), k, me).start()
                return 0

            lax.fori_loop(1, owners, send, 0)

    loads[0].wait()
    for f in range(frames - 1, 1, -1):
        lift(f)
        if f == frames - 1:
            send_on(2)
    loads[1].wait()
    for s in range(halves - 1, 1, -1):
        reduce_frame(s)
    take(0)
    lift(1)
    reduce_frame(1)
    loads[2].wait()
    for s in range(halves - 1, 0, -1):
        convolve(s)
        scatter(s)
    take(1)
    lift(0)
    take(2)
    reduce_frame(0)
    convolve(0)
    scatter(0)
    for load in loads[3:]:
        load.wait()

    place = lax.broadcasted_iota(jnp.int32, (rows, rows), 0)
    other = lax.broadcasted_iota(jnp.int32, (rows, rows), 1)
    allowed = (lax.rem(place, pixels) == lax.rem(other, pixels)) & (other <= place)

    for c in range(chunks):
        for s in range(halves):
            held[c, me, s] = spatial[s, me * chunks + c]

        def arrive(k, _):
            source = lax.rem(me + owners - k, owners)
            for s in range(halves):
                outward(s, c, lax.rem(me + k, owners), k, source).wait_recv()
            return 0

        lax.fori_loop(1, owners, arrive, 0)
        wide = held[c].reshape(rows, channels).astype(f32)
        scale = lax.rsqrt(jnp.mean(wide * wide, axis=-1, keepdims=True) + epsilon)
        normed = (wide * scale * gain[...]).astype(bf16)
        query = jnp.dot(normed, wq[...], preferred_element_type=f32).astype(bf16)
        key = jnp.dot(normed, wk[...], preferred_element_type=f32).astype(bf16)
        value = jnp.dot(normed, wv[...], preferred_element_type=f32).astype(bf16)
        scores = lax.dot_general(
            query, key, (((1,), (1,)), ((), ())), preferred_element_type=f32
        ) * channels ** (-0.5)
        scores = jnp.where(allowed, scores, -1e30)
        largest = jnp.max(scores, axis=-1, keepdims=True)
        probs = jnp.exp(scores - largest)
        probs = (probs / jnp.sum(probs, axis=-1, keepdims=True)).astype(bf16)
        context = jnp.dot(probs, value, preferred_element_type=f32).astype(bf16)
        mixed = jnp.dot(context, wo[...], preferred_element_type=f32)
        result = (wide + mixed).astype(bf16)
        done[c] = result.reshape(owners, halves, pixels, channels)

        def back(k, _):
            homeward(c, lax.rem(me + k, owners), k, me).start()
            return 0

        lax.fori_loop(1, owners, back, 0)
        y_ref[:, me, c] = done[c, me]

    @pl.when(has_next)
    def _():
        for i in range(3):
            onward(i).wait_send()

    for s in range(halves):
        for side in range(2):
            @pl.when(sends_side[side])
            def _():
                sideways(s, side).wait_send()

    for c in range(chunks):
        def finish(k, _):
            peer, source = lax.rem(me + k, owners), lax.rem(me + owners - k, owners)
            for s in range(halves):
                outward(s, c, peer, k, me).wait_send()
            homeward(c, peer, k, me).wait_send()
            homeward(c, peer, k, source).wait_recv()
            return 0

        lax.fori_loop(1, owners, finish, 0)


def per_device(
    video, w_time, b_time, w_down, b_down, w_space, b_space, gain, w_query, w_key, w_value, w_out
):
    frames, height, strip, channels = video.shape
    halves, owners, area = frames // 2, lax.axis_size("tm"), height * strip
    owned = area // owners
    pixels = min(16, owned)
    chunks = owned // pixels
    vmem = pl.BlockSpec(memory_space=pltpu.VMEM)
    hbm = pl.BlockSpec(memory_space=pl.ANY)
    bf16 = jnp.bfloat16
    square = (channels, channels)
    shifted = pltpu.VMEM((halves, height + 2, strip, channels), bf16)
    flat = lambda v: v.reshape(1, channels)
    sems = pltpu.SemaphoreType.DMA
    result = pl.pallas_call(
        partial(block_kernel, (height, strip)),
        out_shape=jax.ShapeDtypeStruct((halves, owners, chunks, pixels, channels), bf16),
        in_specs=[vmem, hbm, vmem, hbm, vmem, hbm, vmem, vmem, hbm, hbm, hbm, hbm],
        out_specs=vmem,
        scratch_shapes=[
            pltpu.VMEM((3,) + square, bf16),
            pltpu.VMEM((3,) + square, bf16),
            pltpu.VMEM((9,) + square, bf16),
            pltpu.VMEM(square, bf16),
            pltpu.VMEM(square, bf16),
            pltpu.VMEM(square, bf16),
            pltpu.VMEM(square, bf16),
            pltpu.VMEM((2, area, channels), bf16),
            pltpu.VMEM((area, channels), bf16),
            pltpu.VMEM((frames, area, channels), bf16),
            shifted,
            shifted,
            shifted,
            pltpu.VMEM((area, channels), jnp.float32),
            pltpu.VMEM((halves, 2, height, channels), bf16),
            pltpu.VMEM((halves, 2, height, channels), bf16),
            pltpu.VMEM((halves, area // pixels, pixels, channels), bf16),
            pltpu.VMEM((chunks, owners, halves, pixels, channels), bf16),
            pltpu.VMEM((chunks, owners, halves, pixels, channels), bf16),
            sems((7,)),
            sems((3,)),
            sems((3,)),
            sems((halves, 2)),
            sems((halves, 2)),
            sems((halves, chunks, owners)),
            sems((halves, chunks, owners)),
            sems((chunks, owners)),
            sems((chunks, owners)),
        ],
        compiler_params=pltpu.CompilerParams(
            collective_id=0, has_side_effects=True, vmem_limit_bytes=56 * 1024 * 1024
        ),
    )(
        video.reshape(frames, area, channels), w_time, flat(b_time), w_down, flat(b_down),
        w_space, flat(b_space), flat(gain), w_query, w_key, w_value, w_out,
    )
    return result.reshape(halves, height, strip, channels)


def solution(mesh):
    return jax.shard_map(
        per_device,
        mesh=mesh,
        in_specs=(P(("clips", "tm"), None, "cols", None),) + (P(),) * 11,
        out_specs=P(("clips", "tm"), None, "cols", None),
        check_vma=False,
    )
```

time: 122 us -> 92.8 us (0.76)
  Pallas kernels: 52.7 us -> 90.3 us
  waiting for transfers between devices: 30.8 us -> 0 us
  matrix products: 13.6 us -> 0 us
  starting transfers between devices: 12.2 us -> 0 us
  local copies, waits for them, and re-layouts: 7.52 us -> 2.26 us
  other arithmetic: 4.26 us -> 0 us
    pallas_call x1, Pallas kernels: 52.7 us -> 90.3 us  [per_device(): pl.pallas_call(partial(block_kernel, (height, strip)), out_shape=jax.Shap...]
    ppermute x4 -> x0, waiting for transfers between devices: 30.8 us -> none  [the longest x2 29.8 us: passed_along(): lax.ppermute(value, axis, [(source, source + steps) for source in range(f...]
    dot_general x18 -> x0, matrix products: 13.6 us -> none  [the longest x9 7.26 us: per_device(): jnp.dot(window.reshape(-1, channels), w_space[3 * row_tap + col_tap], pre...]
    ppermute x4 -> x0, starting transfers between devices: 12.2 us -> none  [the longest x2 9.38 us: passed_along(): lax.ppermute(value, axis, [(source, source + steps) for source in range(f...]
    slice x5 -> x0, local copies, waits for them, and re-layouts: 3.81 us -> none  [the longest x1 2.3 us: temporal(): window = extended[first - offset:first - offset + count]]
    concatenate x4 -> x0, other arithmetic: 2.42 us -> none  [the longest x2 2.06 us: padded(): x = jnp.concatenate([before, x, after], axis=dim)]
    convert_element_type x2 -> x0, other arithmetic: 1.84 us -> none  [the longest x1 1.18 us: lift(): (extended[first:first + count].astype(jnp.float32) + jax.nn.silu(summed))...]
    unnamed x27 -> x1, local copies, waits for them, and re-layouts: 3.71 us -> 2.26 us
  transfers between devices with their start and end apart: 4 -> 0, of which waited for: 3 -> 0; matrix products, arithmetic and copies ran while one was open for 3% -> 0% of each run, Pallas kernels for 0% -> 0%
where the time goes in v2:
time: 92.8 us; the launch traced here: 92.6 us
  Pallas kernels  90.3 us (97%)
  local copies, waits for them, and re-layouts  2.26 us (2%)
    pallas_call x1, Pallas kernels, per_device(): pl.pallas_call(partial(block_kernel, (height, strip)), out_shape=jax.Shap...  90.3 us
    unnamed x1, local copies, waits for them, and re-layouts  2.26 us

profile of v2, /device:TPU:0, one launch (start us, length us, event | category | flops | bytes accessed | tf_op | source)
XLA Modules:
  0.0 92.6 jit_solution(2271690872290154699)
XLA Ops:
  0.0 90.3 %shard_map.118 = bf16[2,8,4,16,512]{4,3,2,1,0:T(8,128)(2,1)} custom-call(bf16[4,512,512]{2,1,0:T(8,128)(2,1)} %bitcast.7, bf16[3,512,512]{2,1,0:T(8,128)(2,1)} %wt_hbm.1, f32[1,512]{1,0:T(1,128)} %bitcast.8, bf16[3,512,512]{2,1,0:T(8,128)(2,1)} %wd_hbm.1, f32[1,512]{1,0:T(1,128)} %bitcast.9, bf16[9,512,512]{2,1,0:T(8,128)(2,1)} %ws_hbm.1, ...), custom_call_target="tpu_custom_call" | custom-call | tf_op jit(solution)/shard_map/pallas_call | solution.py:314
  90.3 2.3 %copy.14 = bf16[2,32,16,512]{3,2,1,0:T(8,128)(2,1)} copy(bf16[2,32,16,512]{3,2,1,0:T(8,128)(2,1)} %bitcast.6) | data formatting | bytes 2097152

commit v3 on v2

v3 whole, which is shorter than its diff:
```python
from functools import partial

import jax
import jax.numpy as jnp
from jax import lax
from jax.experimental import pallas as pl
from jax.experimental.pallas import tpu as pltpu
from jax.sharding import PartitionSpec as P

epsilon = 1e-06
MESH = pl.DeviceIdType.MESH


def block_kernel(
    shape, video_hbm, wt_hbm, bt, wd_hbm, bd, ws_hbm, bs, gain, wq_hbm, wk_hbm, wv_hbm, wo_hbm, y_ref,
    wt, wd, ws, wq, wk, wv, wo, video, lifted, left_of, middle, right_of,
    edges, halo, spatial, held, done,
    load_sem, frame_send, frame_recv, edge_send, edge_recv, send_sem, recv_sem, back_sem, home_sem,
):
    height, strip = shape
    frames, area, channels = video_hbm.shape
    halves, chunks, owners, pixels, _ = y_ref.shape
    total = owners * halves
    rows = total * pixels
    me, col, cols = lax.axis_index("tm"), lax.axis_index("cols"), lax.axis_size("cols")
    f32, bf16 = jnp.float32, jnp.bfloat16
    tile = owners * pixels
    lines = tile // strip

    loads = [
        pltpu.make_async_copy(source, target, load_sem.at[i])
        for i, (source, target) in enumerate(
            (
                (video_hbm, video.at[pl.ds(2, frames)]), (wt_hbm, wt), (wd_hbm, wd), (ws_hbm, ws),
                (wq_hbm, wq), (wk_hbm, wk), (wv_hbm, wv), (wo_hbm, wo),
            )
        )
    ]
    for load in loads:
        load.start()

    barrier = pltpu.get_barrier_semaphore()

    def greet(k, _):
        peer = lax.rem(me + k, owners)
        pl.semaphore_signal(barrier, inc=1, device_id={"tm": peer}, device_id_type=MESH)
        return 0

    lax.fori_loop(1, owners, greet, 0)

    def greet_side(k, _):
        peer = lax.rem(col + k, cols)
        pl.semaphore_signal(barrier, inc=1, device_id={"cols": peer}, device_id_type=MESH)
        return 0

    lax.fori_loop(1, cols, greet_side, 0)
    pl.semaphore_wait(barrier, owners + cols - 2)

    has_next, has_before = me < owners - 1, me > 0

    def span(b):
        return pl.ds(b * tile, tile)

    def landing(i, b):
        return (video.at[1, span(b)], video.at[0, span(b)], lifted.at[0, span(b)])[i]

    def onward(i, b):
        source = (video.at[frames + 1, span(b)], video.at[frames, span(b)], lifted.at[frames, span(b)])[i]
        return pltpu.make_async_remote_copy(
            src_ref=source, dst_ref=landing(i, b),
            send_sem=frame_send.at[i, b], recv_sem=frame_recv.at[i, b],
            device_id={"tm": lax.rem(me + 1, owners)}, device_id_type=MESH,
        )

    def send_on(i, b):
        @pl.when(has_next)
        def _():
            onward(i, b).start()

    def take(i, b):
        @pl.when(has_before)
        def _():
            onward(i, b).wait_recv()

        @pl.when(jnp.logical_not(has_before))
        def _():
            landing(i, b)[...] = jnp.zeros((tile, channels), bf16)

    def stacked(ref, which, b):
        return jnp.concatenate([ref[f, span(b)] for f in which], 0)

    def lift(first, count, b):
        own = [f + 2 for f in range(first, first + count)]
        summed = jnp.dot(stacked(video, own, b), wt[0], preferred_element_type=f32)
        for k in (1, 2):
            summed = summed + jnp.dot(
                stacked(video, [f - k for f in own], b), wt[k], preferred_element_type=f32
            )
        summed = summed + bt[...]
        result = (stacked(video, own, b).astype(f32) + jax.nn.silu(summed)).astype(bf16)
        for i in range(count):
            lifted[first + 1 + i, span(b)] = result[i * tile : (i + 1) * tile]

    def sideways(b, side):
        peer = lax.rem(col + 1, cols) if side == 0 else lax.rem(col + cols - 1, cols)
        return pltpu.make_async_remote_copy(
            src_ref=edges.at[b, side], dst_ref=halo.at[b, side],
            send_sem=edge_send.at[b, side], recv_sem=edge_recv.at[b, side],
            device_id={"cols": peer}, device_id_type=MESH,
        )

    sends_side = (col < cols - 1, col > 0)
    takes_side = (col > 0, col < cols - 1)

    def window(ref, b, a):
        start = b * lines + a
        return ref[:, start : start + lines].reshape(halves * tile, channels)

    def place_band(ref, b, value):
        ref[:, 1 + b * lines : 1 + (b + 1) * lines] = value.reshape(halves, lines, strip, channels)

    def reduce_band(b):
        summed = jnp.zeros((halves * tile, channels), f32) + bd[...]
        for k in range(3):
            which = [2 * s + 2 - k for s in range(halves)]
            summed = summed + jnp.dot(stacked(lifted, which, b), wd[k], preferred_element_type=f32)
        reduced = summed.astype(bf16)
        place_band(middle, b, reduced)
        wide = reduced.astype(f32).reshape(halves, lines, strip, channels)
        edges[b, 0] = wide[:, :, strip - 1].astype(bf16)
        edges[b, 1] = wide[:, :, 0].astype(bf16)
        for side in range(2):
            @pl.when(sends_side[side])
            def _():
                sideways(b, side).start()

    def shift_band(b):
        for side in range(2):
            @pl.when(takes_side[side])
            def _():
                sideways(b, side).wait_recv()

            @pl.when(jnp.logical_not(takes_side[side]))
            def _():
                halo[b, side] = jnp.zeros((halves, lines, channels), bf16)

        size = halves * tile
        wide = window(middle, b, 1).astype(f32)
        place = lax.rem(lax.broadcasted_iota(jnp.int32, (size, channels), 0), strip)

        def spread(side):
            column = halo[b, side].astype(f32)
            column = jnp.broadcast_to(column[:, :, None, :], (halves, lines, strip, channels))
            return column.reshape(size, channels)

        lower = jnp.where(place == 0, spread(0), pltpu.roll(wide, 1, 0))
        upper = jnp.where(place == strip - 1, spread(1), pltpu.roll(wide, size - 1, 0))
        place_band(left_of, b, lower.astype(bf16))
        place_band(right_of, b, upper.astype(bf16))

    def convolve_band(b):
        summed = jnp.zeros((halves * tile, channels), f32) + bs[...]
        for k, shifted in ((1, middle), (0, left_of), (2, right_of)):
            for a in range(3):
                summed = summed + jnp.dot(
                    window(shifted, b, a), ws[3 * a + k], preferred_element_type=f32
                )
        result = (window(middle, b, 1).astype(f32) + jax.nn.silu(summed)).astype(bf16)
        spatial[b] = result.reshape(halves, owners, pixels, channels)

    def outward(c, peer, slot, source):
        return pltpu.make_async_remote_copy(
            src_ref=spatial.at[c, :, peer],
            dst_ref=held.at[c, source],
            send_sem=send_sem.at[c, slot],
            recv_sem=recv_sem.at[c, source],
            device_id={"tm": peer},
            device_id_type=MESH,
        )

    def homeward(c, peer, slot, source):
        return pltpu.make_async_remote_copy(
            src_ref=done.at[c, peer],
            dst_ref=y_ref.at[:, c, source],
            send_sem=back_sem.at[c, slot],
            recv_sem=home_sem.at[c, source],
            device_id={"tm": peer},
            device_id_type=MESH,
        )

    def scatter(c):
        def send(k, _):
            outward(c, lax.rem(me + k, owners), k, me).start()
            return 0

        lax.fori_loop(1, owners, send, 0)

    def attend(c):
        held[c, me] = spatial[c, :, me]

        def arrive(k, _):
            source = lax.rem(me + owners - k, owners)
            outward(c, lax.rem(me + k, owners), k, source).wait_recv()
            return 0

        lax.fori_loop(1, owners, arrive, 0)
        place = lax.broadcasted_iota(jnp.int32, (rows, rows), 0)
        other = lax.broadcasted_iota(jnp.int32, (rows, rows), 1)
        allowed = (lax.rem(place, pixels) == lax.rem(other, pixels)) & (other <= place)
        wide = held[c].reshape(rows, channels).astype(f32)
        scale = lax.rsqrt(jnp.mean(wide * wide, axis=-1, keepdims=True) + epsilon)
        normed = (wide * scale * gain[...]).astype(bf16)
        query = jnp.dot(normed, wq[...], preferred_element_type=f32).astype(bf16)
        key = jnp.dot(normed, wk[...], preferred_element_type=f32).astype(bf16)
        value = jnp.dot(normed, wv[...], preferred_element_type=f32).astype(bf16)
        scores = lax.dot_general(
            query, key, (((1,), (1,)), ((), ())), preferred_element_type=f32
        ) * channels ** (-0.5)
        scores = jnp.where(allowed, scores, -1e30)
        largest = jnp.max(scores, axis=-1, keepdims=True)
        probs = jnp.exp(scores - largest)
        probs = (probs / jnp.sum(probs, axis=-1, keepdims=True)).astype(bf16)
        context = jnp.dot(probs, value, preferred_element_type=f32).astype(bf16)
        mixed = jnp.dot(context, wo[...], preferred_element_type=f32)
        result = (wide + mixed).astype(bf16)
        done[c] = result.reshape(owners, halves, pixels, channels)

        def back(k, _):
            homeward(c, lax.rem(me + k, owners), k, me).start()
            return 0

        lax.fori_loop(1, owners, back, 0)
        y_ref[:, c, me] = done[c, me]

    for shifted in (left_of, middle, right_of):
        for line in (0, height + 1):
            shifted[:, line] = jnp.zeros((halves, strip, channels), bf16)
    loads[0].wait()
    send_on(0, 0)
    send_on(1, 0)
    loads[1].wait()
    for b in range(chunks):
        lift(2, frames - 2, b)
        send_on(2, b)
        if b + 1 < chunks:
            send_on(0, b + 1)
            send_on(1, b + 1)
    for load in loads[2:]:
        load.wait()
    for b in range(chunks + 1):
        if b < chunks:
            take(0, b)
            take(1, b)
            lift(0, 2, b)
            take(2, b)
            reduce_band(b)
            if b >= 2:
                attend(b - 2)
            shift_band(b)
        if b >= 1:
            convolve_band(b - 1)
            scatter(b - 1)
    for c in range(max(0, chunks - 2), chunks):
        attend(c)

    @pl.when(has_next)
    def _():
        for b in range(chunks):
            for i in range(3):
                onward(i, b).wait_send()

    for b in range(chunks):
        for side in range(2):
            @pl.when(sends_side[side])
            def _():
                sideways(b, side).wait_send()

    for c in range(chunks):
        def finish(k, _):
            peer, source = lax.rem(me + k, owners), lax.rem(me + owners - k, owners)
            outward(c, peer, k, me).wait_send()
            homeward(c, peer, k, me).wait_send()
            homeward(c, peer, k, source).wait_recv()
            return 0

        lax.fori_loop(1, owners, finish, 0)


def per_device(
    video, w_time, b_time, w_down, b_down, w_space, b_space, gain, w_query, w_key, w_value, w_out
):
    frames, height, strip, channels = video.shape
    halves, owners, area = frames // 2, lax.axis_size("tm"), height * strip
    owned = area // owners
    pixels = min(16, owned)
    chunks = owned // pixels
    vmem = pl.BlockSpec(memory_space=pltpu.VMEM)
    hbm = pl.BlockSpec(memory_space=pltpu.HBM)
    bf16 = jnp.bfloat16
    square = (channels, channels)
    shifted = pltpu.VMEM((halves, height + 2, strip, channels), bf16)
    flat = lambda v: v.reshape(1, channels)
    sems = pltpu.SemaphoreType.DMA
    result = pl.pallas_call(
        partial(block_kernel, (height, strip)),
        out_shape=jax.ShapeDtypeStruct((halves, chunks, owners, pixels, channels), bf16),
        in_specs=[hbm, hbm, vmem, hbm, vmem, hbm, vmem, vmem, hbm, hbm, hbm, hbm],
        out_specs=vmem,
        scratch_shapes=[
            pltpu.VMEM((3,) + square, bf16),
            pltpu.VMEM((3,) + square, bf16),
            pltpu.VMEM((9,) + square, bf16),
            pltpu.VMEM(square, bf16),
            pltpu.VMEM(square, bf16),
            pltpu.VMEM(square, bf16),
            pltpu.VMEM(square, bf16),
            pltpu.VMEM((frames + 2, area, channels), bf16),
            pltpu.VMEM((frames + 1, area, channels), bf16),
            shifted,
            shifted,
            shifted,
            pltpu.VMEM((chunks, 2, halves, height // chunks, channels), bf16),
            pltpu.VMEM((chunks, 2, halves, height // chunks, channels), bf16),
            pltpu.VMEM((chunks, halves, owners, pixels, channels), bf16),
            pltpu.VMEM((chunks, owners, halves, pixels, channels), bf16),
            pltpu.VMEM((chunks, owners, halves, pixels, channels), bf16),
            sems((8,)),
            sems((3, chunks)),
            sems((3, chunks)),
            sems((chunks, 2)),
            sems((chunks, 2)),
            sems((chunks, owners)),
            sems((chunks, owners)),
            sems((chunks, owners)),
            sems((chunks, owners)),
        ],
        compiler_params=pltpu.CompilerParams(
            collective_id=0, has_side_effects=True, vmem_limit_bytes=44 * 1024 * 1024
        ),
    )(
        video.reshape(frames, area, channels), w_time, flat(b_time), w_down, flat(b_down),
        w_space, flat(b_space), flat(gain), w_query, w_key, w_value, w_out,
    )
    return result.reshape(halves, height, strip, channels)


def solution(mesh):
    return jax.shard_map(
        per_device,
        mesh=mesh,
        in_specs=(P(("clips", "tm"), None, "cols", None),) + (P(),) * 11,
        out_specs=P(("clips", "tm"), None, "cols", None),
        check_vma=False,
    )
```

time: 92.8 us -> 103 us (1.11)
  local copies, waits for them, and re-layouts: 2.26 us -> 12.3 us
    unnamed x1 -> x23, local copies, waits for them, and re-layouts: 2.26 us -> 12.3 us
where the time goes in v3:
time: 103 us; the launch traced here: 102 us
  Pallas kernels  90.1 us (87%)
  local copies, waits for them, and re-layouts  12.3 us (12%)
    pallas_call x1, Pallas kernels, per_device(): pl.pallas_call(partial(block_kernel, (height, strip)), out_shape=jax.Shap...  90.1 us
    unnamed x23, local copies, waits for them, and re-layouts  12.3 us

profile of v3, /device:TPU:0, one launch (start us, length us, event | category | flops | bytes accessed | tf_op | source)
XLA Modules:
  0.0 102.3 jit_solution(9326413408079566731)
XLA Ops:
  0.0 0.0 copy-start
  0.0 1.6 %copy-done = bf16[4,32,16,512]{3,2,1,0:T(8,128)(2,1)S(1)} copy-done((bf16[4,32,16,512]{3,2,1,0:T(8,128)(2,1)S(1)}, bf16[4,32,16,512]{3,2,1,0:T(8,128)(2,1)}, u32[]{:S(2)}) %copy-start) | copy-done | bytes 2097176
  1.6 0.0 copy-start.1
  1.6 1.4 %copy-done.1 = bf16[3,512,512]{2,1,0:T(8,128)(2,1)S(1)} copy-done((bf16[3,512,512]{2,1,0:T(8,128)(2,1)S(1)}, bf16[3,512,512]{2,1,0:T(8,128)(2,1)}, u32[]{:S(2)}) %copy-start.1) | copy-done | bytes 1572888
  3.0 0.0 copy-start.2
  3.0 1.4 %copy-done.2 = bf16[3,512,512]{2,1,0:T(8,128)(2,1)S(1)} copy-done((bf16[3,512,512]{2,1,0:T(8,128)(2,1)S(1)}, bf16[3,512,512]{2,1,0:T(8,128)(2,1)}, u32[]{:S(2)}) %copy-start.2) | copy-done | bytes 1572888
  4.4 0.0 copy-start.3
  4.4 1.0 %copy-done.3 = bf16[512,512]{1,0:T(8,128)(2,1)S(1)} copy-done((bf16[512,512]{1,0:T(8,128)(2,1)S(1)}, bf16[512,512]{1,0:T(8,128)(2,1)}, u32[]{:S(2)}) %copy-start.3) | copy-done | bytes 524312
  5.5 0.0 copy-start.4
  5.5 1.0 %copy-done.4 = bf16[512,512]{1,0:T(8,128)(2,1)S(1)} copy-done((bf16[512,512]{1,0:T(8,128)(2,1)S(1)}, bf16[512,512]{1,0:T(8,128)(2,1)}, u32[]{:S(2)}) %copy-start.4) | copy-done | bytes 524312
  6.5 0.0 copy-start.5
  6.5 1.0 %copy-done.5 = bf16[512,512]{1,0:T(8,128)(2,1)S(1)} copy-done((bf16[512,512]{1,0:T(8,128)(2,1)S(1)}, bf16[512,512]{1,0:T(8,128)(2,1)}, u32[]{:S(2)}) %copy-start.5) | copy-done | bytes 524312
  7.5 0.0 copy-start.6
  7.5 1.0 %copy-done.6 = bf16[512,512]{1,0:T(8,128)(2,1)S(1)} copy-done((bf16[512,512]{1,0:T(8,128)(2,1)S(1)}, bf16[512,512]{1,0:T(8,128)(2,1)}, u32[]{:S(2)}) %copy-start.6) | copy-done | bytes 524312
  8.6 0.0 copy-start.7
  8.6 0.7 copy-done.7
  9.3 0.0 copy-start.8
  9.3 0.7 copy-done.8
  9.9 0.0 copy-start.9
  9.9 0.7 copy-done.9
  10.6 0.0 copy-start.10
  10.6 0.7 copy-done.10
  11.3 90.1 %shard_map.118 = bf16[2,4,8,16,512]{4,3,2,1,0:T(8,128)(2,1)S(1)} custom-call(bf16[4,512,512]{2,1,0:T(8,128)(2,1)S(1)} %bitcast.7, bf16[3,512,512]{2,1,0:T(8,128)(2,1)S(1)} %copy-done.1, f32[1,512]{1,0:T(1,128)S(1)} %bitcast.8, bf16[3,512,512]{2,1,0:T(8,128)(2,1)S(1)} %copy-done.2, f32[1,512]{1,0:T(1,128)S(1)} %bitcast.9, bf16[9,512,512]{2,1,0:T(8,128)(2,1)} %ws_hbm.1, ...), custom_call_target="tpu_custom_call" | custom-call | tf_op jit(solution)/shard_map/pallas_call | solution.py:304
  101.4 1.0 copy.14
Async XLA Ops:
  0.0 1.6 %copy-start = (bf16[4,32,16,512]{3,2,1,0:T(8,128)(2,1)S(1)}, bf16[4,32,16,512]{3,2,1,0:T(8,128)(2,1)}, u32[]{:S(2)}) copy-start(bf16[4,32,16,512]{3,2,1,0:T(8,128)(2,1)} %param.12) | copy-start | bytes 6291460
  1.6 1.4 %copy-start.1 = (bf16[3,512,512]{2,1,0:T(8,128)(2,1)S(1)}, bf16[3,512,512]{2,1,0:T(8,128)(2,1)}, u32[]{:S(2)}) copy-start(bf16[3,512,512]{2,1,0:T(8,128)(2,1)} %wt_hbm.1) | copy-start | bytes 4718596
  3.0 1.4 %copy-start.2 = (bf16[3,512,512]{2,1,0:T(8,128)(2,1)S(1)}, bf16[3,512,512]{2,1,0:T(8,128)(2,1)}, u32[]{:S(2)}) copy-start(bf16[3,512,512]{2,1,0:T(8,128)(2,1)} %wd_hbm.1) | copy-start | bytes 4718596
  4.4 1.0 %copy-start.3 = (bf16[512,512]{1,0:T(8,128)(2,1)S(1)}, bf16[512,512]{1,0:T(8,128)(2,1)}, u32[]{:S(2)}) copy-start(bf16[512,512]{1,0:T(8,128)(2,1)} %wq_hbm.1) | copy-start | bytes 1572868
  5.5 1.0 %copy-start.4 = (bf16[512,512]{1,0:T(8,128)(2,1)S(1)}, bf16[512,512]{1,0:T(8,128)(2,1)}, u32[]{:S(2)}) copy-start(bf16[512,512]{1,0:T(8,128)(2,1)} %wk_hbm.1) | copy-start | bytes 1572868
  6.5 1.0 %copy-start.5 = (bf16[512,512]{1,0:T(8,128)(2,1)S(1)}, bf16[512,512]{1,0:T(8,128)(2,1)}, u32[]{:S(2)}) copy-start(bf16[512,512]{1,0:T(8,128)(2,1)} %wv_hbm.1) | copy-start | bytes 1572868
  7.5 1.0 %copy-start.6 = (bf16[512,512]{1,0:T(8,128)(2,1)S(1)}, bf16[512,512]{1,0:T(8,128)(2,1)}, u32[]{:S(2)}) copy-start(bf16[512,512]{1,0:T(8,128)(2,1)} %wo_hbm.1) | copy-start | bytes 1572868
  8.6 0.7 copy-start.7
  9.3 0.7 copy-start.8
  9.9 0.7 copy-start.9
  10.6 0.7 copy-start.10

commit v4 on v3

--- a/solution.py
+++ b/solution.py
@@ -254,13 +254,11 @@
             lift(0, 2, b)
             take(2, b)
             reduce_band(b)
-            if b >= 2:
-                attend(b - 2)
             shift_band(b)
         if b >= 1:
             convolve_band(b - 1)
             scatter(b - 1)
-    for c in range(max(0, chunks - 2), chunks):
+    for c in range(chunks):
         attend(c)
 
     @pl.when(has_next)

time: 103 us -> 99.3 us (0.964)
  Pallas kernels: 90.1 us -> 86.5 us
    pallas_call x1, Pallas kernels: 90.1 us -> 86.5 us  [per_device(): pl.pallas_call(partial(block_kernel, (height, strip)), out_shape=jax.Shap...]
where the time goes in v4:
time: 99.3 us; the launch traced here: 98.8 us
  Pallas kernels  86.5 us (87%)
  local copies, waits for them, and re-layouts  12.3 us (12%)
    pallas_call x1, Pallas kernels, per_device(): pl.pallas_call(partial(block_kernel, (height, strip)), out_shape=jax.Shap...  86.5 us
    unnamed x23, local copies, waits for them, and re-layouts  12.3 us

profile of v4, /device:TPU:0, one launch (start us, length us, event | category | flops | bytes accessed | tf_op | source)
XLA Modules:
  0.0 98.8 jit_solution(9586035197388106377)
XLA Ops:
  0.0 0.0 copy-start
  0.0 1.6 %copy-done = bf16[4,32,16,512]{3,2,1,0:T(8,128)(2,1)S(1)} copy-done((bf16[4,32,16,512]{3,2,1,0:T(8,128)(2,1)S(1)}, bf16[4,32,16,512]{3,2,1,0:T(8,128)(2,1)}, u32[]{:S(2)}) %copy-start) | copy-done | bytes 2097176
  1.6 0.0 copy-start.1
  1.6 1.4 %copy-done.1 = bf16[3,512,512]{2,1,0:T(8,128)(2,1)S(1)} copy-done((bf16[3,512,512]{2,1,0:T(8,128)(2,1)S(1)}, bf16[3,512,512]{2,1,0:T(8,128)(2,1)}, u32[]{:S(2)}) %copy-start.1) | copy-done | bytes 1572888
  3.0 0.0 copy-start.2
  3.0 1.4 %copy-done.2 = bf16[3,512,512]{2,1,0:T(8,128)(2,1)S(1)} copy-done((bf16[3,512,512]{2,1,0:T(8,128)(2,1)S(1)}, bf16[3,512,512]{2,1,0:T(8,128)(2,1)}, u32[]{:S(2)}) %copy-start.2) | copy-done | bytes 1572888
  4.4 0.0 copy-start.3
  4.4 1.0 %copy-done.3 = bf16[512,512]{1,0:T(8,128)(2,1)S(1)} copy-done((bf16[512,512]{1,0:T(8,128)(2,1)S(1)}, bf16[512,512]{1,0:T(8,128)(2,1)}, u32[]{:S(2)}) %copy-start.3) | copy-done | bytes 524312
  5.5 0.0 copy-start.4
  5.5 1.0 %copy-done.4 = bf16[512,512]{1,0:T(8,128)(2,1)S(1)} copy-done((bf16[512,512]{1,0:T(8,128)(2,1)S(1)}, bf16[512,512]{1,0:T(8,128)(2,1)}, u32[]{:S(2)}) %copy-start.4) | copy-done | bytes 524312
  6.5 0.0 copy-start.5
  6.5 1.0 %copy-done.5 = bf16[512,512]{1,0:T(8,128)(2,1)S(1)} copy-done((bf16[512,512]{1,0:T(8,128)(2,1)S(1)}, bf16[512,512]{1,0:T(8,128)(2,1)}, u32[]{:S(2)}) %copy-start.5) | copy-done | bytes 524312
  7.5 0.0 copy-start.6
  7.5 1.0 %copy-done.6 = bf16[512,512]{1,0:T(8,128)(2,1)S(1)} copy-done((bf16[512,512]{1,0:T(8,128)(2,1)S(1)}, bf16[512,512]{1,0:T(8,128)(2,1)}, u32[]{:S(2)}) %copy-start.6) | copy-done | bytes 524312
  8.6 0.0 copy-start.7
  8.6 0.7 copy-done.7
  9.3 0.0 copy-start.8
  9.3 0.7 copy-done.8
  9.9 0.0 copy-start.9
  9.9 0.7 copy-done.9
  10.6 0.0 copy-start.10
  10.6 0.7 copy-done.10
  11.3 86.5 %shard_map.118 = bf16[2,4,8,16,512]{4,3,2,1,0:T(8,128)(2,1)S(1)} custom-call(bf16[4,512,512]{2,1,0:T(8,128)(2,1)S(1)} %bitcast.7, bf16[3,512,512]{2,1,0:T(8,128)(2,1)S(1)} %copy-done.1, f32[1,512]{1,0:T(1,128)S(1)} %bitcast.8, bf16[3,512,512]{2,1,0:T(8,128)(2,1)S(1)} %copy-done.2, f32[1,512]{1,0:T(1,128)S(1)} %bitcast.9, bf16[9,512,512]{2,1,0:T(8,128)(2,1)} %ws_hbm.1, ...), custom_call_target="tpu_custom_call" | custom-call | tf_op jit(solution)/shard_map/pallas_call | solution.py:302
  97.8 1.0 copy.14
Async XLA Ops:
  0.0 1.6 %copy-start = (bf16[4,32,16,512]{3,2,1,0:T(8,128)(2,1)S(1)}, bf16[4,32,16,512]{3,2,1,0:T(8,128)(2,1)}, u32[]{:S(2)}) copy-start(bf16[4,32,16,512]{3,2,1,0:T(8,128)(2,1)} %param.12) | copy-start | bytes 6291460
  1.6 1.4 %copy-start.1 = (bf16[3,512,512]{2,1,0:T(8,128)(2,1)S(1)}, bf16[3,512,512]{2,1,0:T(8,128)(2,1)}, u32[]{:S(2)}) copy-start(bf16[3,512,512]{2,1,0:T(8,128)(2,1)} %wt_hbm.1) | copy-start | bytes 4718596
  3.0 1.4 %copy-start.2 = (bf16[3,512,512]{2,1,0:T(8,128)(2,1)S(1)}, bf16[3,512,512]{2,1,0:T(8,128)(2,1)}, u32[]{:S(2)}) copy-start(bf16[3,512,512]{2,1,0:T(8,128)(2,1)} %wd_hbm.1) | copy-start | bytes 4718596
  4.4 1.0 %copy-start.3 = (bf16[512,512]{1,0:T(8,128)(2,1)S(1)}, bf16[512,512]{1,0:T(8,128)(2,1)}, u32[]{:S(2)}) copy-start(bf16[512,512]{1,0:T(8,128)(2,1)} %wq_hbm.1) | copy-start | bytes 1572868
  5.5 1.0 %copy-start.4 = (bf16[512,512]{1,0:T(8,128)(2,1)S(1)}, bf16[512,512]{1,0:T(8,128)(2,1)}, u32[]{:S(2)}) copy-start(bf16[512,512]{1,0:T(8,128)(2,1)} %wk_hbm.1) | copy-start | bytes 1572868
  6.5 1.0 %copy-start.5 = (bf16[512,512]{1,0:T(8,128)(2,1)S(1)}, bf16[512,512]{1,0:T(8,128)(2,1)}, u32[]{:S(2)}) copy-start(bf16[512,512]{1,0:T(8,128)(2,1)} %wv_hbm.1) | copy-start | bytes 1572868
  7.5 1.0 %copy-start.6 = (bf16[512,512]{1,0:T(8,128)(2,1)S(1)}, bf16[512,512]{1,0:T(8,128)(2,1)}, u32[]{:S(2)}) copy-start(bf16[512,512]{1,0:T(8,128)(2,1)} %wo_hbm.1) | copy-start | bytes 1572868
  8.6 0.7 copy-start.7
  9.3 0.7 copy-start.8
  9.9 0.7 copy-start.9
  10.6 0.7 copy-start.10

commit v5 on v4

--- a/solution.py
+++ b/solution.py
@@ -333,7 +333,7 @@
             sems((chunks, owners)),
         ],
         compiler_params=pltpu.CompilerParams(
-            collective_id=0, has_side_effects=True, vmem_limit_bytes=44 * 1024 * 1024
+            collective_id=0, has_side_effects=True, vmem_limit_bytes=57 * 1024 * 1024
         ),
     )(
         video.reshape(frames, area, channels), w_time, flat(b_time), w_down, flat(b_down),

time: 99.3 us -> 90.1 us (0.907)
  local copies, waits for them, and re-layouts: 12.3 us -> 2.26 us
  Pallas kernels: 86.5 us -> 87.6 us
    unnamed x23 -> x1, local copies, waits for them, and re-layouts: 12.3 us -> 2.26 us
    pallas_call x1, Pallas kernels: 86.5 us -> 87.6 us  [per_device(): pl.pallas_call(partial(block_kernel, (height, strip)), out_shape=jax.Shap...]
where the time goes in v5:
time: 90.1 us; the launch traced here: 89.9 us
  Pallas kernels  87.6 us (97%)
  local copies, waits for them, and re-layouts  2.26 us (3%)
    pallas_call x1, Pallas kernels, per_device(): pl.pallas_call(partial(block_kernel, (height, strip)), out_shape=jax.Shap...  87.6 us
    unnamed x1, local copies, waits for them, and re-layouts  2.26 us

profile of v5, /device:TPU:0, one launch (start us, length us, event | category | flops | bytes accessed | tf_op | source)
XLA Modules:
  0.0 89.9 jit_solution(8282929760612518658)
XLA Ops:
  0.0 87.6 %shard_map.118 = bf16[2,4,8,16,512]{4,3,2,1,0:T(8,128)(2,1)} custom-call(bf16[4,512,512]{2,1,0:T(8,128)(2,1)} %bitcast.7, bf16[3,512,512]{2,1,0:T(8,128)(2,1)} %wt_hbm.1, f32[1,512]{1,0:T(1,128)} %bitcast.8, bf16[3,512,512]{2,1,0:T(8,128)(2,1)} %wd_hbm.1, f32[1,512]{1,0:T(1,128)} %bitcast.9, bf16[9,512,512]{2,1,0:T(8,128)(2,1)} %ws_hbm.1, ...), custom_call_target="tpu_custom_call" | custom-call | tf_op jit(solution)/shard_map/pallas_call | solution.py:302
  87.7 2.3 %copy.14 = bf16[2,32,16,512]{3,2,1,0:T(8,128)(2,1)} copy(bf16[2,32,16,512]{3,2,1,0:T(8,128)(2,1)} %bitcast.6) | data formatting | bytes 2097152

commit v6 on v5

--- a/solution.py
+++ b/solution.py
@@ -256,9 +256,11 @@
             reduce_band(b)
             shift_band(b)
         if b >= 1:
+            if b == chunks and chunks > 1:
+                attend(0)
             convolve_band(b - 1)
             scatter(b - 1)
-    for c in range(chunks):
+    for c in range(min(1, chunks - 1), chunks):
         attend(c)
 
     @pl.when(has_next)

time: 90.1 us -> 89.4 us (level)
  no operation moved by 1% of the time
where the time goes in v6:
time: 89.4 us; the launch traced here: 89.1 us
  Pallas kernels  86.8 us (97%)
  local copies, waits for them, and re-layouts  2.26 us (3%)
    pallas_call x1, Pallas kernels, per_device(): pl.pallas_call(partial(block_kernel, (height, strip)), out_shape=jax.Shap...  86.8 us
    unnamed x1, local copies, waits for them, and re-layouts  2.26 us

profile of v6, /device:TPU:0, one launch (start us, length us, event | category | flops | bytes accessed | tf_op | source)
XLA Modules:
  0.0 89.1 jit_solution(11506931904988292138)
XLA Ops:
  0.0 86.8 %shard_map.118 = bf16[2,4,8,16,512]{4,3,2,1,0:T(8,128)(2,1)} custom-call(bf16[4,512,512]{2,1,0:T(8,128)(2,1)} %bitcast.7, bf16[3,512,512]{2,1,0:T(8,128)(2,1)} %wt_hbm.1, f32[1,512]{1,0:T(1,128)} %bitcast.8, bf16[3,512,512]{2,1,0:T(8,128)(2,1)} %wd_hbm.1, f32[1,512]{1,0:T(1,128)} %bitcast.9, bf16[9,512,512]{2,1,0:T(8,128)(2,1)} %ws_hbm.1, ...), custom_call_target="tpu_custom_call" | custom-call | tf_op jit(solution)/shard_map/pallas_call | solution.py:304
  86.8 2.3 %copy.14 = bf16[2,32,16,512]{3,2,1,0:T(8,128)(2,1)} copy(bf16[2,32,16,512]{3,2,1,0:T(8,128)(2,1)} %bitcast.6) | data formatting | bytes 2097152
